TPU v7x, 32 devices: a whole 2x2x4 slice. The times are simulated.
32 devices in a mesh: replica: 8 (over y, x, core), tensor: 4 (over z).
Axes of the slice: x: 2, y: 2, z: 4, core: 2. Of those that a mesh axis runs over, the one named last changes fastest.
Arguments:
- weights: bfloat16 [8, 8192, 2048], P('replica', 'tensor'), may hold values from -6 to 6
- hidden: bfloat16 [8, 512, 8192], P('replica', None, 'tensor'), may hold values from -6 to 6
- out_grad: bfloat16 [8, 512, 2048], P('replica', None, 'tensor'), may hold values from -0.375 to 0.375
- factor_start: bfloat16 [2, 64, 8192], P(None, None, 'tensor'), may hold values from -6 to 6
- matching: int32 [2], replicated, may hold values from 1 to 7, as said below
Outputs:
- new_weights: bfloat16 [8, 8192, 2048], P('replica', 'tensor')
Inputs may be any that keep to these rules, and one draw needn't show every extreme that they name: In step t replica i is matched with replica i XOR matching[t]; in one of the steps matching equals 7.
All inputs are finite; a program needn't handle non-finite values.
Results may differ from a plain program's by a relative error of at most 0.014.
Values may be sent and summed in bfloat16 or wider, within the bound.
No kernel may reach another device: no remote copies, remote signals or barrier semaphores. Data moves between devices by JAX's collectives and lax.ppermute only.
A program may use at most 128 MiB of HBM per device.

v0:
```python
import functools

import jax
import jax.numpy as jnp
from jax import lax
from jax.experimental import pallas as pl
from jax.experimental.pallas import tpu as pltpu
from jax.sharding import PartitionSpec as P

learn_rate = 0.1
momentum_decay = 0.9
older_share = learn_rate * (1.0 + momentum_decay)
bf16 = jnp.bfloat16
f32 = jnp.float32

VMEM = pl.BlockSpec(memory_space=pltpu.VMEM)
SMEM = pl.BlockSpec(memory_space=pltpu.SMEM)
HBM = pl.BlockSpec(memory_space=pltpu.HBM)
room = pltpu.CompilerParams(vmem_limit_bytes=28 * 2**20)


def dot(a, b, contract, precision=None):
    return lax.dot_general(
        a, b, (((contract[0],), (contract[1],)), ((), ())),
        precision=precision, preferred_element_type=f32,
    )


def exact(a, b, contract):
    return dot(a, b, contract, lax.Precision.HIGHEST)


def columns_of(place, width):
    return pl.ds(pl.multiple_of(place * width, width), width)


def write_pieces(out, parts, seen):
    at = 0
    for part in parts:
        out[:, at : at + part.shape[1]] = part
        at += part.shape[1]
    out[:, at:] = seen


def project_kernel(count, tokens, me_ref, f_hbm, h_hbm, w_hbm, kept, sent, w, h, f, total, sems):
    rank = kept.shape[0]
    span = w.shape[1] // count
    chunks = 4
    size = w.shape[0] // chunks
    first = pltpu.make_async_copy(f_hbm, f, sems.at[chunks])
    first.start()
    copies = []
    for i in range(chunks):
        at = pl.ds(i * size, size)
        copies.append(pltpu.make_async_copy(w_hbm.at[at], w.at[at], sems.at[i]))
        copies[-1].start()
    last = pltpu.make_async_copy(h_hbm, h, sems.at[chunks + 1])
    last.start()
    first.wait()
    for i in range(chunks):
        copies[i].wait()
        part = dot(f[:, i * size : (i + 1) * size], w[i * size : (i + 1) * size, :], (1, 0))
        total[...] = part if i == 0 else total[...] + part
    last.wait()
    both = dot(f[...], h[...], (1, 1)).astype(bf16)
    seen = jnp.concatenate(
        [both[:rank, :tokens], both[rank:, :tokens], both[rank:, tokens:]], 1
    )
    for out, start in ((kept, 0), (sent, 1)):
        parts = []
        for r in range(start, count, 2):
            part = total[:, columns_of(me_ref[0] ^ r, span)].astype(bf16)
            parts += [part[:rank], part[rank:]]
        write_pieces(out, parts, seen)


def project(me, factors, h, w, count, rank, tokens):
    _, depth = w.shape
    span = depth // count
    length = count * span + 3 * tokens
    message = jax.ShapeDtypeStruct((rank, length), bf16)
    return pl.pallas_call(
        functools.partial(project_kernel, count, tokens),
        in_specs=[SMEM, HBM, HBM, HBM],
        out_specs=[VMEM] * 2,
        out_shape=[message, message],
        scratch_shapes=[
            pltpu.VMEM(w.shape, bf16),
            pltpu.VMEM(h.shape, bf16),
            pltpu.VMEM(factors.shape, bf16),
            pltpu.VMEM((2 * rank, depth), f32),
            pltpu.SemaphoreType.DMA((6,)),
        ],
        compiler_params=room,
        name="project",
    )(me, *(pltpu.with_memory_space_constraint(x, pltpu.HBM) for x in (factors, h, w)))


def halve(kept, arrived, tokens, span):
    rank, length = kept.shape
    pieces = (length - 3 * tokens) // (2 * span)
    message = jax.ShapeDtypeStruct((rank, pieces * span + 3 * tokens), bf16)

    def kernel(kept, arrived, keep, send):
        total = (kept[...].astype(f32) + arrived[...].astype(f32)).astype(bf16)
        for out, start in ((keep, 0), (send, 1)):
            parts = [total[:, 2 * span * r : 2 * span * (r + 1)] for r in range(start, pieces, 2)]
            write_pieces(out, parts, total[:, 2 * span * pieces :])

    return pl.pallas_call(
        kernel, out_shape=[message] * 2, in_specs=[VMEM] * 2, out_specs=[VMEM] * 2,
        compiler_params=room, name="halve",
    )(kept, arrived)


def left_kernel(count, tokens, g_ref, *refs):
    messages, (mine, left) = refs[:count], refs[count:]
    span = g_ref.shape[1]
    total = messages[0][...].astype(f32)
    for k in range(1, count):
        total = total + messages[k][...].astype(f32)
    seen = total[:, 2 * span :].astype(bf16)
    older = dot(seen[:, tokens : 2 * tokens], g_ref[:tokens, :], (1, 0))
    mine[:, :span] = (
        total[:, :span] - learn_rate * dot(seen[:, :tokens], g_ref[:tokens, :], (1, 0))
    ).astype(bf16)
    later = total[:, span : 2 * span] - learn_rate * older
    mine[:, span:] = later.astype(bf16)
    left[...] = later - learn_rate * (
        momentum_decay * older + dot(seen[:, 2 * tokens :], g_ref[tokens:, :], (1, 0))
    )


def left_products(g, messages, tokens):
    rank, span = messages[0].shape[0], g.shape[1]
    return pl.pallas_call(
        functools.partial(left_kernel, len(messages), tokens),
        out_shape=[
            jax.ShapeDtypeStruct((rank, 2 * span), bf16),
            jax.ShapeDtypeStruct((rank, span), f32),
        ],
        in_specs=[VMEM] * (1 + len(messages)),
        out_specs=[VMEM] * 2,
        compiler_params=room,
        name="left",
    )(g, *messages)


def differ_kernel(mine, other, out):
    _, length = mine.shape
    span = length // 2
    diff = (mine[:, :span].astype(f32) - other[:, :span].astype(f32)).astype(bf16)
    both = (mine[:, span:].astype(f32) + other[:, span:].astype(f32)).astype(bf16)
    out[:, :span] = diff
    out[:, span:] = dot(both, diff, (1, 1)).astype(bf16)


def differ(mine, other):
    rank, length = mine.shape
    return pl.pallas_call(
        differ_kernel,
        out_shape=jax.ShapeDtypeStruct((rank, length // 2 + rank), bf16),
        in_specs=[VMEM] * 2,
        out_specs=VMEM,
        compiler_params=room,
        name="differ",
    )(mine, other)


def inverse_factor(gram):
    size = gram.shape[0]
    work = gram
    rows = lax.broadcasted_iota(jnp.int32, (size, size), 0)
    columns = lax.broadcasted_iota(jnp.int32, (size, size), 1)
    scale = jnp.ones((size, size), f32)
    for k in range(size):
        pivot_row = work[k : k + 1, :]
        pivot = work[k : k + 1, k : k + 1]
        row = jnp.where(columns[:1] == k, 1.0, pivot_row) / pivot
        ratio = jnp.where(rows > k, work[:, k : k + 1], 0.0)
        kept = jnp.where((columns == k) & (rows > k), 0.0, work)
        work = kept - ratio * row
        scale = jnp.where(rows == k, pivot, scale)
    lower = jnp.where(rows > columns, work, jnp.where(rows == columns, 1.0, 0.0))
    return lower * lax.rsqrt(scale)


def ortho_first_kernel(count, me_ref, left_ref, *refs):
    messages, (ortho, out, whole) = refs[:count], refs[count:]
    rank, span = left_ref.shape
    edge = jnp.zeros((rank, rank), f32)
    for k in range(count):
        place = lax.rem(me_ref[0] + count - k, count)
        whole[:, columns_of(place, span)] = messages[k][:, :span]
        edge = edge + messages[k][:, span:].astype(f32)
    inverse = inverse_factor(dot(whole[...], whole[...], (1, 1)))
    near = exact(inverse, messages[0][:, :span].astype(f32), (1, 0)).astype(bf16)
    turned = exact(edge, inverse, (1, 1)).astype(bf16)
    out[...] = (left_ref[...] - 0.5 * dot(turned, near, (1, 0))).astype(bf16)
    ortho[...] = exact(inverse, whole[...].astype(f32), (1, 0)).astype(bf16)


def ortho_first(me, left, messages):
    count = len(messages)
    rank, span = left.shape
    return pl.pallas_call(
        functools.partial(ortho_first_kernel, count),
        out_shape=[
            jax.ShapeDtypeStruct((rank, span * count), bf16),
            jax.ShapeDtypeStruct((rank, span), bf16),
        ],
        in_specs=[SMEM] + [VMEM] * (1 + count),
        out_specs=[VMEM] * 2,
        scratch_shapes=[pltpu.VMEM((rank, span * count), bf16)],
        compiler_params=room,
        name="ortho_first",
    )(me, left, *messages)


def ortho_second_kernel(whole, ortho, inverse):
    inverse[...] = inverse_factor(dot(whole[...], whole[...], (1, 1)))
    ortho[...] = exact(inverse[...], whole[...].astype(f32), (1, 0)).astype(bf16)


def ortho_second(whole):
    rank = whole.shape[0]
    return pl.pallas_call(
        ortho_second_kernel,
        out_shape=[jax.ShapeDtypeStruct(whole.shape, bf16), jax.ShapeDtypeStruct((rank, rank), f32)],
        in_specs=[VMEM],
        out_specs=[VMEM] * 2,
        compiler_params=room,
        name="ortho_second",
    )(whole)


def right_first_kernel(count, me_ref, ortho, h, w, *refs):
    grads, (out,) = refs[:count], refs[count:]
    tokens = h.shape[0] // 2
    span = grads[0].shape[1]
    total = jnp.zeros((ortho.shape[0], tokens), f32)
    for k in range(count):
        place = lax.rem(me_ref[0] + count - k, count)
        total = total + dot(ortho[:, columns_of(place, span)], grads[k][...], (1, 1))
    seen = (learn_rate * total).astype(bf16)
    out[...] = (
        dot(ortho[...], w[...], (1, 1)) - dot(seen, h[:tokens, :], (1, 0))
    ).astype(bf16)


def right_first(me, ortho, h, w, grads):
    return pl.pallas_call(
        functools.partial(right_first_kernel, len(grads)),
        in_specs=[SMEM] + [VMEM] * (3 + len(grads)),
        out_specs=VMEM,
        out_shape=jax.ShapeDtypeStruct((ortho.shape[0], w.shape[0]), bf16),
        compiler_params=room,
        name="right_first",
    )(me, ortho, h, w, *grads)


def descend_kernel(count, size, me_ref, h, w_hbm, *refs):
    grads, (out, w, u, loads, stores) = refs[:count], refs[count:]
    tokens, span = grads[0].shape
    blocks = w.shape[0] // size

    def load(i):
        at = pl.ds(i * size, size)
        return pltpu.make_async_copy(w_hbm.at[at], w.at[at], loads.at[i])

    def store(i):
        at = pl.ds(i * size, size)
        return pltpu.make_async_copy(u.at[at], out.at[at], stores.at[i])

    for i in range(blocks):
        load(i).start()

    def body(i, _):
        rows = pl.ds(pl.multiple_of(i * size, size), size)
        turned = (older_share * h[:tokens, rows].astype(f32)).astype(bf16).T
        load(i).wait()
        for k in range(count):
            at = columns_of(lax.rem(me_ref[0] + count - k, count), span)
            u[rows, at] = (
                w[rows, at].astype(f32) - dot(turned, grads[k][...], (1, 0))
            ).astype(bf16)
        store(i).start()
        return 0

    lax.fori_loop(0, blocks, body, 0)
    for i in range(blocks):
        store(i).wait()


def descend(me, h, w, grads):
    size = min(256, w.shape[0])
    blocks = w.shape[0] // size
    return pl.pallas_call(
        functools.partial(descend_kernel, len(grads), size),
        in_specs=[SMEM, VMEM, HBM] + [VMEM] * len(grads),
        out_specs=HBM,
        out_shape=jax.ShapeDtypeStruct(w.shape, bf16),
        scratch_shapes=[pltpu.VMEM(w.shape, bf16)] * 2
        + [pltpu.SemaphoreType.DMA((blocks,))] * 2,
        compiler_params=room,
        name="descend",
    )(me, h, pltpu.with_memory_space_constraint(w, pltpu.HBM), *grads)


def right_second_kernel(count, me_ref, before, h, w, mine, other, *refs):
    messages, olds, news = (refs[j * count : (j + 1) * count] for j in range(3))
    out, whole = refs[3 * count :]
    tokens = h.shape[0] // 2
    span = messages[0].shape[1]
    older = newer = jnp.zeros((before.shape[0], tokens), f32)
    for k in range(count):
        place = lax.rem(me_ref[0] + count - k, count)
        whole[:, columns_of(place, span)] = messages[k][...]
        older = older + dot(messages[k][...], olds[k][...], (1, 1))
        newer = newer + dot(messages[k][...], news[k][...], (1, 1))
    older = (older_share * older).astype(bf16)
    newer = (learn_rate * newer).astype(bf16)
    turned = (0.5 * dot(whole[...], before[...], (1, 1))).astype(bf16)
    turn = (mine[...].astype(f32) - other[...].astype(f32)).astype(bf16)
    out[...] = (
        dot(whole[...], w[...], (1, 1))
        - dot(jnp.concatenate([older, newer], 1), h[...], (1, 0))
        - dot(turned, turn, (1, 0))
    ).astype(bf16)


def right_second(me, before, h, w, mine, other, messages, olds, news):
    rank, depth = before.shape
    return pl.pallas_call(
        functools.partial(right_second_kernel, len(messages)),
        in_specs=[SMEM] + [VMEM] * (5 + 3 * len(messages)),
        out_specs=[VMEM] * 2,
        out_shape=[
            jax.ShapeDtypeStruct((rank, w.shape[0]), bf16),
            jax.ShapeDtypeStruct((rank, depth), bf16),
        ],
        compiler_params=room,
        name="right_second",
    )(me, before, h, w, mine, other, *messages, *olds, *news)


def move_kernel(count, me_ref, first, second, inverse, u, h, a0, b0, a1, b1, *refs):
    grads, (out, turn, ortho, block, sems) = refs[:count], refs[count:]
    rank = first.shape[0]
    tokens = h.shape[0] // 2
    span = grads[0].shape[1]
    size = min(256, u.shape[0])
    turn[:rank, :] = (0.5 * (a0[...].astype(f32) - b0[...].astype(f32))).astype(bf16)
    turn[rank : 2 * rank, :] = (
        0.5 * exact(inverse[...], a1[...].astype(f32) - b1[...].astype(f32), (1, 0))
    ).astype(bf16)
    turn[2 * rank :, :] = (learn_rate * h[tokens:, :].astype(f32)).astype(bf16)
    ortho[:rank, :] = first[...]
    ortho[rank : 2 * rank, :] = second[...]
    for k in range(count):
        at = columns_of(lax.rem(me_ref[0] + count - k, count), span)
        ortho[2 * rank :, at] = grads[k][...]
    copies = []
    for i in range(u.shape[0] // size):
        rows = slice(i * size, (i + 1) * size)
        block[rows, :] = (
            u[rows, :].astype(f32) - dot(turn[:, rows].T, ortho[...], (1, 0))
        ).astype(bf16)
        at = pl.ds(i * size, size)
        copies.append(pltpu.make_async_copy(block.at[at], out.at[at], sems.at[i]))
        copies[-1].start()
    for copy in copies:
        copy.wait()


def move(me, first, second, inverse, u, h, pairs, grads):
    rank = first.shape[0]
    tokens = h.shape[0] // 2
    depth = 2 * rank + tokens
    blocks = u.shape[0] // min(256, u.shape[0])
    return pl.pallas_call(
        functools.partial(move_kernel, len(grads)),
        in_specs=[SMEM] + [VMEM] * (9 + len(grads)),
        out_specs=HBM,
        out_shape=jax.ShapeDtypeStruct(u.shape, bf16),
        scratch_shapes=[
            pltpu.VMEM((depth, u.shape[0]), bf16),
            pltpu.VMEM((depth, u.shape[1]), bf16),
            pltpu.VMEM(u.shape, bf16),
            pltpu.SemaphoreType.DMA((blocks,)),
        ],
        compiler_params=room,
        name="move",
    )(me, first, second, inverse, u, h, *pairs, *grads)


def swap(value, which, beside=None):
    count = lax.axis_size("replica")

    def branch(x, mask):
        arrived = lax.ppermute(x, "replica", [(s, s ^ mask) for s in range(count)])
        return arrived, (beside() if beside else ())

    branches = [functools.partial(branch, mask=mask) for mask in range(1, count)]
    arrived, extra = lax.switch(which - 1, branches, value)
    return (arrived, extra) if beside else arrived


def shift(value, step):
    count = lax.axis_size("tensor")
    return lax.ppermute(value, "tensor", [(s, (s + step) % count) for s in range(count)])


def across(value, bit):
    count = lax.axis_size("tensor")
    return lax.ppermute(value, "tensor", [(s, s ^ bit) for s in range(count)])


def spread(value):
    count = lax.axis_size("tensor")
    return [value] + [shift(value, k) for k in range(1, count)]


def after(value, *events):
    return lax.optimization_barrier((value, *events))[0]


def per_device(weights, hidden, out_grad, factor_start, matching):
    return both_steps(weights[0], hidden[0], out_grad[0], factor_start, matching)[None]


def both_steps(w, h, g, factor_start, matching):
    count = lax.axis_size("tensor")
    me = lax.axis_index("tensor").astype(jnp.int32).reshape(1)
    steps, rank, width = factor_start.shape
    tokens = g.shape[0] // steps
    span = g.shape[1]

    first, second = [g[:tokens]], [g[tokens:]]
    first.append(shift(first[0], 1))
    kept, sent = project(
        me, factor_start.reshape(steps * rank, width), h, w, count, rank, tokens
    )
    bit = 1
    while True:
        arrived = across(sent, bit)
        bit *= 2
        if bit == count:
            break
        kept, sent = halve(kept, arrived, tokens, span)
    mine, left = left_products(g, [kept, arrived], tokens)
    first.append(shift(after(first[1], mine), 1))
    second.append(shift(after(second[0], mine), 1))
    other = swap(mine, matching[0])
    message = differ(mine, other)
    messages = spread(message)
    ortho0, left = ortho_first(me, left, messages)
    for _ in range(3, count):
        first.append(shift(after(first[-1], messages[-1]), 1))
    second.append(shift(after(second[1], messages[-1]), 1))
    other = swap(left, matching[1])
    diff = (left.astype(f32) - other.astype(f32)).astype(bf16)
    pieces = spread(diff)
    right0 = right_first(me, after(ortho0, diff), h, w, first)
    for _ in range(3, count):
        second.append(shift(after(second[-1], diff), 1))
    other0, u = swap(right0, matching[0], lambda: descend(me, h, w, first))
    right1, whole = right_second(me, ortho0, h, w, right0, other0, pieces, first, second)
    other1, (ortho1, inverse1) = swap(right1, matching[1], lambda: ortho_second(whole))
    return move(me, ortho0, ortho1, inverse1, u, h, (right0, other0, right1, other1), second)


def solution(mesh):
    return jax.shard_map(
        per_device,
        mesh=mesh,
        in_specs=(
            P("replica", "tensor", None),
            P("replica", None, "tensor"),
            P("replica", None, "tensor"),
            P(None, None, "tensor"),
            P(),
        ),
        out_specs=P("replica", "tensor", None),
        check_vma=False,
    )
```

profile of v0, /device:TPU:1, one launch (start us, length us, event | category | flops | bytes accessed | tf_op | source)
XLA Modules:
  0.0 130.3 jit_solution(11430267867650538300)
XLA Ops:
  0.0 5.2 %project.1 = (bf16[64,2816]{1,0:T(8,128)(2,1)S(1)}, bf16[64,2816]{1,0:T(8,128)(2,1)S(1)}) custom-call(s32[1]{0:T(128)} %bitcast.me_ref, bf16[128,2048]{1,0:T(8,128)(2,1)} %bitcast.34, bf16[512,2048]{1,0:T(8,128)(2,1)} %bitcast.23, bf16[2048,2048]{1,0:T(8,128)(2,1)} %bitcast.13), custom_call_target="tpu_custom_call" | custom-call | tf_op jit(solution)/shard_map/project/pallas_call | solution.py:82
  5.2 2.2 %collective-permute-start.28 = (bf16[64,2816]{1,0:T(8,128)(2,1)S(1)}, bf16[64,2816]{1,0:T(8,128)(2,1)S(1)}, u32[]{:S(2)}, u32[]{:S(2)}) collective-permute-start(bf16[64,2816]{1,0:T(8,128)(2,1)S(1)} %get-tuple-element.286), channel_id=1, source_target_pairs={{0,1},{1,0},{2,3},{3,2},{4,5},{5,4},{6,7},{7,6},{8,9},{9,8},{10,11... | collective-permute-start | bytes 1081352 | tf_op jit(solution)/shard_map/ppermute | solution.py:416
  7.4 8.1 %collective-permute-done.28.arrived = bf16[64,2816]{1,0:T(8,128)(2,1)S(1)} collective-permute-done((bf16[64,2816]{1,0:T(8,128)(2,1)S(1)}, bf16[64,2816]{1,0:T(8,128)(2,1)S(1)}, u32[]{:S(2)}, u32[]{:S(2)}) %collective-permute-start.28) | collective-permute-done | bytes 360480 | tf_op jit(solution)/shard_map/ppermute | solution.py:416
  15.6 2.3 %collective-permute-start.29 = (bf16[64,1792]{1,0:T(8,128)(2,1)S(1)}, bf16[64,1792]{1,0:T(8,128)(2,1)S(1)}, u32[]{:S(2)}, u32[]{:S(2)}) collective-permute-start(bf16[64,1792]{1,0:T(8,128)(2,1)S(1)} %get-tuple-element.288), channel_id=1, source_target_pairs={{0,2},{1,3},{2,0},{3,1},{4,6},{5,7},{6,4},{7,5},{8,10},{9,11},{10,... | collective-permute-start | bytes 688136 | tf_op jit(solution)/shard_map/ppermute | solution.py:416
  17.9 1.3 %collective-permute-start.33 = (bf16[256,512]{1,0:T(8,128)(2,1)S(1)}, bf16[256,512]{1,0:T(8,128)(2,1)S(1)}, u32[]{:S(2)}, u32[]{:S(2)}) collective-permute-start(bf16[256,512]{1,0:T(8,128)(2,1)S(1)} %get-tuple-element.306.refs_0_.refs_4_), channel_id=1, source_target_pairs={{0,1},{1,2},{2,3},{3,0},{4,5},{5,6},{6,7},{7,4},{8,9},{9,10},{10,1... | collective-permute-start | bytes 786440 | tf_op jit(solution)/shard_map/ppermute | solution.py:411
  19.2 14.5 %collective-permute-done.29.refs_1_ = bf16[64,1792]{1,0:T(8,128)(2,1)S(1)} collective-permute-done((bf16[64,1792]{1,0:T(8,128)(2,1)S(1)}, bf16[64,1792]{1,0:T(8,128)(2,1)S(1)}, u32[]{:S(2)}, u32[]{:S(2)}) %collective-permute-start.29) | collective-permute-done | bytes 229408 | tf_op jit(solution)/shard_map/ppermute | solution.py:416
  34.1 0.9 collective-permute-start.34
  34.9 0.6 fusion
  36.1 7.3 %conditional.7 = (bf16[64,1024]{1,0:T(8,128)(2,1)}) conditional(s32[]{:T(128)} %bitcast.5, bf16[64,1024]{1,0:T(8,128)(2,1)S(1)} %get-tuple-element.290.mine, bf16[64,1024]{1,0:T(8,128)(2,1)S(1)} %get-tuple-element.290.mine, bf16[64,1024]{1,0:T(8,128)(2,1)S(1)} %get-tuple-element.290.mine, ...), branch_computations={%region_0.0_spmd, %region_1.0_spmd, %region_2.0_spmd, %region_3.0_... | conditional | bytes 524336 | solution.py:405
  36.2 3.0 %collective-permute-start.6 = (bf16[64,1024]{1,0:T(8,128)(2,1)S(1)}, bf16[64,1024]{1,0:T(8,128)(2,1)}, u32[]{:S(2)}, u32[]{:S(2)}) collective-permute-start(bf16[64,1024]{1,0:T(8,128)(2,1)S(1)} %param.6), channel_id=1, source_target_pairs={{0,28},{4,24},{8,20},{12,16},{16,12},{20,8},{24,4},{28,0},{1,29},{... | collective-permute-start | bytes 393224 | tf_op jit(solution)/shard_map/cond/branch_6_fun/ppermute | solution.py:401
  39.1 4.3 %collective-permute-done.6 = bf16[64,1024]{1,0:T(8,128)(2,1)} collective-permute-done((bf16[64,1024]{1,0:T(8,128)(2,1)S(1)}, bf16[64,1024]{1,0:T(8,128)(2,1)}, u32[]{:S(2)}, u32[]{:S(2)}) %collective-permute-start.6) | collective-permute-done | bytes 131104 | tf_op jit(solution)/shard_map/cond/branch_6_fun/ppermute | solution.py:401
  43.4 1.1 differ.1.refs_0_
  44.5 3.4 %collective-permute-start.32 = (bf16[64,576]{1,0:T(8,128)(2,1)S(1)}, bf16[64,576]{1,0:T(8,128)(2,1)S(1)}, u32[]{:S(2)}, u32[]{:S(2)}) collective-permute-start(bf16[64,576]{1,0:T(8,128)(2,1)S(1)} %differ.1.refs_0_), channel_id=1, source_target_pairs={{0,3},{1,0},{2,1},{3,2},{4,7},{5,4},{6,5},{7,6},{8,11},{9,8},{10,9... | collective-permute-start | bytes 221192 | tf_op jit(solution)/shard_map/ppermute | solution.py:411
  47.9 2.0 %collective-permute-start.31 = (bf16[64,576]{1,0:T(8,128)(2,1)S(1)}, bf16[64,576]{1,0:T(8,128)(2,1)S(1)}, u32[]{:S(2)}, u32[]{:S(2)}) collective-permute-start(bf16[64,576]{1,0:T(8,128)(2,1)S(1)} %differ.1.refs_0_), channel_id=1, source_target_pairs={{0,2},{1,3},{2,0},{3,1},{4,6},{5,7},{6,4},{7,5},{8,10},{9,11},{10,... | collective-permute-start | bytes 221192 | tf_op jit(solution)/shard_map/ppermute | solution.py:411
  49.8 1.7 %collective-permute-done.32.refs_3_ = bf16[64,576]{1,0:T(8,128)(2,1)S(1)} collective-permute-done((bf16[64,576]{1,0:T(8,128)(2,1)S(1)}, bf16[64,576]{1,0:T(8,128)(2,1)S(1)}, u32[]{:S(2)}, u32[]{:S(2)}) %collective-permute-start.32) | collective-permute-done | bytes 73760 | tf_op jit(solution)/shard_map/ppermute | solution.py:411
  52.2 1.0 collective-permute-done.30.refs_1_
  53.2 6.5 %ortho_first.1 = (bf16[64,2048]{1,0:T(8,128)(2,1)S(1)}, bf16[64,512]{1,0:T(8,128)(2,1)S(1)}) custom-call(s32[1]{0:T(128)} %bitcast.me_ref, f32[64,512]{1,0:T(8,128)S(1)} %get-tuple-element.289.left_ref, bf16[64,576]{1,0:T(8,128)(2,1)S(1)} %differ.1.refs_0_, bf16[64,576]{1,0:T(8,128)(2,1)S(1)} %collective-permute-done.30.refs_1_, ...), custom_call_target="tpu_custom_call" | custom-call | tf_op jit(solution)/shard_map/ortho_first/pallas_call | solution.py:206
  59.7 5.9 %conditional.8 = (bf16[64,512]{1,0:T(8,128)(2,1)}) conditional(s32[]{:T(128)} %bitcast.6, bf16[64,512]{1,0:T(8,128)(2,1)S(1)} %get-tuple-element.292, bf16[64,512]{1,0:T(8,128)(2,1)S(1)} %get-tuple-element.292, bf16[64,512]{1,0:T(8,128)(2,1)S(1)} %get-tuple-element.292, ...), branch_computations={%region_7.0_spmd, %region_8.0_spmd, %region_9.0_spmd, %region_10.0... | conditional | bytes 262192
  59.7 4.2 %collective-permute-start.10 = (bf16[64,512]{1,0:T(8,128)(2,1)S(1)}, bf16[64,512]{1,0:T(8,128)(2,1)}, u32[]{:S(2)}, u32[]{:S(2)}) collective-permute-start(bf16[64,512]{1,0:T(8,128)(2,1)S(1)} %param.10), channel_id=1, source_target_pairs={{0,16},{4,20},{8,24},{12,28},{16,0},{20,4},{24,8},{28,12},{1,17},{... | collective-permute-start | bytes 196616 | tf_op jit(solution)/shard_map/cond/branch_3_fun/ppermute | solution.py:401
  63.8 1.8 %collective-permute-done.10 = bf16[64,512]{1,0:T(8,128)(2,1)} collective-permute-done((bf16[64,512]{1,0:T(8,128)(2,1)S(1)}, bf16[64,512]{1,0:T(8,128)(2,1)}, u32[]{:S(2)}, u32[]{:S(2)}) %collective-permute-start.10) | collective-permute-done | bytes 65568 | tf_op jit(solution)/shard_map/cond/branch_3_fun/ppermute | solution.py:401
  65.6 0.9 subtract_convert_fusion.refs_0_
  66.5 0.3 collective-permute-start.41
  66.8 3.0 %collective-permute-start.36 = (bf16[64,512]{1,0:T(8,128)(2,1)S(1)}, bf16[64,512]{1,0:T(8,128)(2,1)S(1)}, u32[]{:S(2)}, u32[]{:S(2)}) collective-permute-start(bf16[64,512]{1,0:T(8,128)(2,1)S(1)} %subtract_convert_fusion.refs_0_), channel_id=1, source_target_pairs={{0,1},{1,2},{2,3},{3,0},{4,5},{5,6},{6,7},{7,4},{8,9},{9,10},{10,1... | collective-permute-start | bytes 196616 | tf_op jit(solution)/shard_map/ppermute | solution.py:411
  70.2 2.3 %collective-permute-start.38 = (bf16[64,512]{1,0:T(8,128)(2,1)S(1)}, bf16[64,512]{1,0:T(8,128)(2,1)S(1)}, u32[]{:S(2)}, u32[]{:S(2)}) collective-permute-start(bf16[64,512]{1,0:T(8,128)(2,1)S(1)} %subtract_convert_fusion.refs_0_), channel_id=1, source_target_pairs={{0,3},{1,0},{2,1},{3,2},{4,7},{5,4},{6,5},{7,6},{8,11},{9,8},{10,9... | collective-permute-start | bytes 196616 | tf_op jit(solution)/shard_map/ppermute | solution.py:411
  72.6 7.1 %right_first.1.mine.a0 = bf16[64,2048]{1,0:T(8,128)(2,1)S(1)} custom-call(s32[1]{0:T(128)} %bitcast.me_ref, bf16[64,2048]{1,0:T(8,128)(2,1)S(1)} %get-tuple-element.293.ortho.before.first, bf16[512,2048]{1,0:T(8,128)(2,1)} %bitcast.24, bf16[2048,2048]{1,0:T(8,128)(2,1)} %bitcast.14, bf16[256,512]{1,0:T(8,128)(2,1)S(1)} %get-tuple-element.306.refs_0_.refs_4_, ...), custom_call_target="tpu_custom_call" | custom-call | tf_op jit(solution)/shard_map/right_first/pallas_call | solution.py:252
  79.8 22.7 %conditional.9 = (bf16[64,2048]{1,0:T(8,128)(2,1)}, bf16[2048,2048]{1,0:T(8,128)(2,1)S(1)}) conditional(s32[]{:T(128)} %bitcast.5, (bf16[64,2048]{1,0:T(8,128)(2,1)S(1)}, s32[1]{0:T(128)}, bf16[512,2048]{1,0:T(8,128)(2,1)}, bf16[2048,2048]{1,0:T(8,128)(2,1)}, bf16[256,512]{1,0:T(8,128)(2,1)S(1)}, ...), branch_computations={%region_14.0_spmd, %region_15.0_spmd, %region_16.0_spmd, %region_1... | conditional | bytes 1048632 | solution.py:405
  79.8 14.6 %collective-permute-start.20 = (bf16[64,2048]{1,0:T(8,128)(2,1)S(1)}, bf16[64,2048]{1,0:T(8,128)(2,1)}, u32[]{:S(2)}, u32[]{:S(2)}) collective-permute-start(bf16[64,2048]{1,0:T(8,128)(2,1)S(1)} %get-tuple-element.229), channel_id=1, source_target_pairs={{0,28},{4,24},{8,20},{12,16},{16,12},{20,8},{24,4},{28,0},{1,29},{... | collective-permute-start | bytes 786440 | tf_op jit(solution)/shard_map/cond/branch_6_fun/ppermute | solution.py:401
  94.5 7.8 %descend.13 = bf16[2048,2048]{1,0:T(8,128)(2,1)S(1)} custom-call(s32[1]{0:T(128)} %get-tuple-element.230.me_ref, bf16[512,2048]{1,0:T(8,128)(2,1)} %get-tuple-element.231.h, bf16[2048,2048]{1,0:T(8,128)(2,1)} %get-tuple-element.232.w_hbm, bf16[256,512]{1,0:T(8,128)(2,1)S(1)} %get-tuple-element.233.refs_0_, bf16[256,512]{1,0:T(8,128)(2,1)S(1)} %get-tuple-element.234.refs_1_, ...), custom_call_target="tpu_custom_call" | custom-call | tf_op jit(solution)/shard_map/cond/branch_6_fun/descend/pallas_call | solution.py:298
  102.5 10.7 %right_second.1 = (bf16[64,2048]{1,0:T(8,128)(2,1)S(1)}, bf16[64,2048]{1,0:T(8,128)(2,1)S(1)}) custom-call(s32[1]{0:T(128)} %bitcast.me_ref, bf16[64,2048]{1,0:T(8,128)(2,1)S(1)} %get-tuple-element.293.ortho.before.first, bf16[512,2048]{1,0:T(8,128)(2,1)} %bitcast.32, bf16[2048,2048]{1,0:T(8,128)(2,1)} %bitcast.22, bf16[64,2048]{1,0:T(8,128)(2,1)S(1)} %right_first.1.mine.a0, ...), custom_call_target="tpu_custom_call" | custom-call | tf_op jit(solution)/shard_map/right_second/pallas_call | solution.py:334
  113.3 6.6 %conditional.10 = (bf16[64,2048]{1,0:T(8,128)(2,1)}, bf16[64,2048]{1,0:T(8,128)(2,1)S(1)}, f32[64,64]{1,0:T(8,128)S(1)}) conditional(s32[]{:T(128)} %bitcast.6, (bf16[64,2048]{1,0:T(8,128)(2,1)S(1)}, bf16[64,2048]{1,0:T(8,128)(2,1)S(1)}) %right_second.1, (bf16[64,2048]{1,0:T(8,128)(2,1)S(1)}, ...), branch_computations={%region_21.0_spmd, %region_22.0_spmd, %region_23.0_spmd, %region_2... | conditional | bytes 1048640 | solution.py:405
  113.4 6.2 %ortho_second.10 = (bf16[64,2048]{1,0:T(8,128)(2,1)S(1)}, f32[64,64]{1,0:T(8,128)S(1)}) custom-call(bf16[64,2048]{1,0:T(8,128)(2,1)S(1)} %get-tuple-element.250.whole), custom_call_target="tpu_custom_call" | custom-call | tf_op jit(solution)/shard_map/cond/branch_3_fun/ortho_second/pallas_call | solution.py:227
  119.8 10.2 %move.1 = bf16[2048,2048]{1,0:T(8,128)(2,1)} custom-call(s32[1]{0:T(128)} %bitcast.me_ref, bf16[64,2048]{1,0:T(8,128)(2,1)S(1)} %get-tuple-element.293.ortho.before.first, bf16[64,2048]{1,0:T(8,128)(2,1)S(1)} %get-tuple-element.300.second, f32[64,64]{1,0:T(8,128)S(1)} %get-tuple-element.301.inverse, bf16[2048,2048]{1,0:T(8,128)(2,1)} %copy-done.1, ...), custom_call_target="tpu_custom_call" | custom-call | tf_op jit(solution)/shard_map/move/pallas_call | solution.py:381
  (27 shorter events, 1.0 us)
Async XLA Ops:
  0.0 17.9 %copy-start = (bf16[1,512,512]{2,1,0:T(8,128)(2,1)S(1)}, bf16[1,512,512]{2,1,0:T(8,128)(2,1)}, u32[]{:S(2)}) copy-start(bf16[1,512,512]{2,1,0:T(8,128)(2,1)} %param.35) | copy-start | bytes 1572868
  0.0 34.9 %copy-start.2 = (s32[2]{0:T(128)S(1)}, s32[2]{0:T(128)}, u32[]{:S(2)}) copy-start(s32[2]{0:T(128)} %param.37) | copy-start | bytes 28
  5.2 10.3 %collective-permute-start.28 = (bf16[64,2816]{1,0:T(8,128)(2,1)S(1)}, bf16[64,2816]{1,0:T(8,128)(2,1)S(1)}, u32[]{:S(2)}, u32[]{:S(2)}) collective-permute-start(bf16[64,2816]{1,0:T(8,128)(2,1)S(1)} %get-tuple-element.286), channel_id=1, source_target_pairs={{0,1},{1,0},{2,3},{3,2},{4,5},{5,4},{6,7},{7,6},{8,9},{9,8},{10,11... | collective-permute-start | bytes 1081352 | tf_op jit(solution)/shard_map/ppermute | solution.py:416
  15.6 18.1 %collective-permute-start.29 = (bf16[64,1792]{1,0:T(8,128)(2,1)S(1)}, bf16[64,1792]{1,0:T(8,128)(2,1)S(1)}, u32[]{:S(2)}, u32[]{:S(2)}) collective-permute-start(bf16[64,1792]{1,0:T(8,128)(2,1)S(1)} %get-tuple-element.288), channel_id=1, source_target_pairs={{0,2},{1,3},{2,0},{3,1},{4,6},{5,7},{6,4},{7,5},{8,10},{9,11},{10,... | collective-permute-start | bytes 688136 | tf_op jit(solution)/shard_map/ppermute | solution.py:416
  17.9 16.2 %collective-permute-start.33 = (bf16[256,512]{1,0:T(8,128)(2,1)S(1)}, bf16[256,512]{1,0:T(8,128)(2,1)S(1)}, u32[]{:S(2)}, u32[]{:S(2)}) collective-permute-start(bf16[256,512]{1,0:T(8,128)(2,1)S(1)} %get-tuple-element.306.refs_0_.refs_4_), channel_id=1, source_target_pairs={{0,1},{1,2},{2,3},{3,0},{4,5},{5,6},{6,7},{7,4},{8,9},{9,10},{10,1... | collective-permute-start | bytes 786440 | tf_op jit(solution)/shard_map/ppermute | solution.py:411
  34.0 17.5 %collective-permute-start.39 = (bf16[256,512]{1,0:T(8,128)(2,1)S(1)}, bf16[256,512]{1,0:T(8,128)(2,1)S(1)}, u32[]{:S(2)}, u32[]{:S(2)}) collective-permute-start(bf16[256,512]{1,0:T(8,128)(2,1)S(1)} %get-tuple-element.297.refs_8_.refs_0_), channel_id=1, source_target_pairs={{0,1},{1,2},{2,3},{3,0},{4,5},{5,6},{6,7},{7,4},{8,9},{9,10},{10,1... | collective-permute-start | bytes 786440 | tf_op jit(solution)/shard_map/ppermute | solution.py:411
  34.1 31.6 %collective-permute-start.34 = (bf16[256,512]{1,0:T(8,128)(2,1)S(1)}, bf16[256,512]{1,0:T(8,128)(2,1)S(1)}, u32[]{:S(2)}, u32[]{:S(2)}) collective-permute-start(bf16[256,512]{1,0:T(8,128)(2,1)S(1)} %collective-permute-done.33.refs_1_.refs_5_), channel_id=1, source_target_pairs={{0,1},{1,2},{2,3},{3,0},{4,5},{5,6},{6,7},{7,4},{8,9},{9,10},{10,1... | collective-permute-start | bytes 786440 | tf_op jit(solution)/shard_map/ppermute | solution.py:411
  36.2 7.2 %collective-permute-start.6 = (bf16[64,1024]{1,0:T(8,128)(2,1)S(1)}, bf16[64,1024]{1,0:T(8,128)(2,1)}, u32[]{:S(2)}, u32[]{:S(2)}) collective-permute-start(bf16[64,1024]{1,0:T(8,128)(2,1)S(1)} %param.6), channel_id=1, source_target_pairs={{0,28},{4,24},{8,20},{12,16},{16,12},{20,8},{24,4},{28,0},{1,29},{... | collective-permute-start | bytes 393224 | tf_op jit(solution)/shard_map/cond/branch_6_fun/ppermute | solution.py:401
  44.5 7.0 %collective-permute-start.32 = (bf16[64,576]{1,0:T(8,128)(2,1)S(1)}, bf16[64,576]{1,0:T(8,128)(2,1)S(1)}, u32[]{:S(2)}, u32[]{:S(2)}) collective-permute-start(bf16[64,576]{1,0:T(8,128)(2,1)S(1)} %differ.1.refs_0_), channel_id=1, source_target_pairs={{0,3},{1,0},{2,1},{3,2},{4,7},{5,4},{6,5},{7,6},{8,11},{9,8},{10,9... | collective-permute-start | bytes 221192 | tf_op jit(solution)/shard_map/ppermute | solution.py:411
  47.9 5.4 %collective-permute-start.30 = (bf16[64,576]{1,0:T(8,128)(2,1)S(1)}, bf16[64,576]{1,0:T(8,128)(2,1)S(1)}, u32[]{:S(2)}, u32[]{:S(2)}) collective-permute-start(bf16[64,576]{1,0:T(8,128)(2,1)S(1)} %differ.1.refs_0_), channel_id=1, source_target_pairs={{0,1},{1,2},{2,3},{3,0},{4,5},{5,6},{6,7},{7,4},{8,9},{9,10},{10,1... | collective-permute-start | bytes 221192 | tf_op jit(solution)/shard_map/ppermute | solution.py:411
  47.9 5.4 %collective-permute-start.31 = (bf16[64,576]{1,0:T(8,128)(2,1)S(1)}, bf16[64,576]{1,0:T(8,128)(2,1)S(1)}, u32[]{:S(2)}, u32[]{:S(2)}) collective-permute-start(bf16[64,576]{1,0:T(8,128)(2,1)S(1)} %differ.1.refs_0_), channel_id=1, source_target_pairs={{0,2},{1,3},{2,0},{3,1},{4,6},{5,7},{6,4},{7,5},{8,10},{9,11},{10,... | collective-permute-start | bytes 221192 | tf_op jit(solution)/shard_map/ppermute | solution.py:411
  51.5 15.0 %collective-permute-start.40 = (bf16[256,512]{1,0:T(8,128)(2,1)S(1)}, bf16[256,512]{1,0:T(8,128)(2,1)S(1)}, u32[]{:S(2)}, u32[]{:S(2)}) collective-permute-start(bf16[256,512]{1,0:T(8,128)(2,1)S(1)} %collective-permute-done.39.refs_9_.refs_1_), channel_id=1, source_target_pairs={{0,1},{1,2},{2,3},{3,0},{4,5},{5,6},{6,7},{7,4},{8,9},{9,10},{10,1... | collective-permute-start | bytes 786440 | tf_op jit(solution)/shard_map/ppermute | solution.py:411
  59.7 5.9 %collective-permute-start.10 = (bf16[64,512]{1,0:T(8,128)(2,1)S(1)}, bf16[64,512]{1,0:T(8,128)(2,1)}, u32[]{:S(2)}, u32[]{:S(2)}) collective-permute-start(bf16[64,512]{1,0:T(8,128)(2,1)S(1)} %param.10), channel_id=1, source_target_pairs={{0,16},{4,20},{8,24},{12,28},{16,0},{20,4},{24,8},{28,12},{1,17},{... | collective-permute-start | bytes 196616 | tf_op jit(solution)/shard_map/cond/branch_3_fun/ppermute | solution.py:401
  65.6 7.0 %collective-permute-start.35 = (bf16[256,512]{1,0:T(8,128)(2,1)S(1)}, bf16[256,512]{1,0:T(8,128)(2,1)S(1)}, u32[]{:S(2)}, u32[]{:S(2)}) collective-permute-start(bf16[256,512]{1,0:T(8,128)(2,1)S(1)} %collective-permute-done.34.refs_2_.refs_6_), channel_id=1, source_target_pairs={{0,1},{1,2},{2,3},{3,0},{4,5},{5,6},{6,7},{7,4},{8,9},{9,10},{10,1... | collective-permute-start | bytes 786440 | tf_op jit(solution)/shard_map/ppermute | solution.py:411
  66.5 36.0 %collective-permute-start.41 = (bf16[256,512]{1,0:T(8,128)(2,1)S(1)}, bf16[256,512]{1,0:T(8,128)(2,1)S(1)}, u32[]{:S(2)}, u32[]{:S(2)}) collective-permute-start(bf16[256,512]{1,0:T(8,128)(2,1)S(1)} %collective-permute-done.40.refs_10_.refs_2_), channel_id=1, source_target_pairs={{0,1},{1,2},{2,3},{3,0},{4,5},{5,6},{6,7},{7,4},{8,9},{9,10},{10,1... | collective-permute-start | bytes 786440 | tf_op jit(solution)/shard_map/ppermute | solution.py:411
  66.8 35.6 %collective-permute-start.36 = (bf16[64,512]{1,0:T(8,128)(2,1)S(1)}, bf16[64,512]{1,0:T(8,128)(2,1)S(1)}, u32[]{:S(2)}, u32[]{:S(2)}) collective-permute-start(bf16[64,512]{1,0:T(8,128)(2,1)S(1)} %subtract_convert_fusion.refs_0_), channel_id=1, source_target_pairs={{0,1},{1,2},{2,3},{3,0},{4,5},{5,6},{6,7},{7,4},{8,9},{9,10},{10,1... | collective-permute-start | bytes 196616 | tf_op jit(solution)/shard_map/ppermute | solution.py:411
  69.9 32.6 %collective-permute-start.37 = (bf16[64,512]{1,0:T(8,128)(2,1)S(1)}, bf16[64,512]{1,0:T(8,128)(2,1)S(1)}, u32[]{:S(2)}, u32[]{:S(2)}) collective-permute-start(bf16[64,512]{1,0:T(8,128)(2,1)S(1)} %subtract_convert_fusion.refs_0_), channel_id=1, source_target_pairs={{0,2},{1,3},{2,0},{3,1},{4,6},{5,7},{6,4},{7,5},{8,10},{9,11},{10,... | collective-permute-start | bytes 196616 | tf_op jit(solution)/shard_map/ppermute | solution.py:411
  70.2 32.3 %collective-permute-start.38 = (bf16[64,512]{1,0:T(8,128)(2,1)S(1)}, bf16[64,512]{1,0:T(8,128)(2,1)S(1)}, u32[]{:S(2)}, u32[]{:S(2)}) collective-permute-start(bf16[64,512]{1,0:T(8,128)(2,1)S(1)} %subtract_convert_fusion.refs_0_), channel_id=1, source_target_pairs={{0,3},{1,0},{2,1},{3,2},{4,7},{5,4},{6,5},{7,6},{8,11},{9,8},{10,9... | collective-permute-start | bytes 196616 | tf_op jit(solution)/shard_map/ppermute | solution.py:411
  79.8 22.4 %collective-permute-start.20 = (bf16[64,2048]{1,0:T(8,128)(2,1)S(1)}, bf16[64,2048]{1,0:T(8,128)(2,1)}, u32[]{:S(2)}, u32[]{:S(2)}) collective-permute-start(bf16[64,2048]{1,0:T(8,128)(2,1)S(1)} %get-tuple-element.229), channel_id=1, source_target_pairs={{0,28},{4,24},{8,20},{12,16},{16,12},{20,8},{24,4},{28,0},{1,29},{... | collective-permute-start | bytes 786440 | tf_op jit(solution)/shard_map/cond/branch_6_fun/ppermute | solution.py:401
  102.5 10.8 %copy-start.1 = (bf16[2048,2048]{1,0:T(8,128)(2,1)}, bf16[2048,2048]{1,0:T(8,128)(2,1)S(1)}, u32[]{:S(2)}) copy-start(bf16[2048,2048]{1,0:T(8,128)(2,1)S(1)} %get-tuple-element.302.u) | copy-start | bytes 25165828
  113.3 6.3 %collective-permute-start.24 = (bf16[64,2048]{1,0:T(8,128)(2,1)S(1)}, bf16[64,2048]{1,0:T(8,128)(2,1)}, u32[]{:S(2)}, u32[]{:S(2)}) collective-permute-start(bf16[64,2048]{1,0:T(8,128)(2,1)S(1)} %get-tuple-element.249), channel_id=1, source_target_pairs={{0,16},{4,20},{8,24},{12,28},{16,0},{20,4},{24,8},{28,12},{1,17},{... | collective-permute-start | bytes 786440 | tf_op jit(solution)/shard_map/cond/branch_3_fun/ppermute | solution.py:401
where the time goes:
time: 131 us; the launch traced here: 130 us
  Pallas kernels  55.1 us (42%)
  starting transfers between devices  39.8 us (30%)
  waiting for transfers between devices  31.6 us (24%)
  between operations  1.63 us (1%)
    ppermute x2, waiting for transfers between devices, across(): return lax.ppermute(value, 'tensor', [(s, s ^ bit) for s in range(count)])  22.6 us
    ppermute x4, starting transfers between devices, branch(): arrived = lax.ppermute(x, 'replica', [(s, s ^ mask) for s in range(count)])  21.8 us
    ppermute x12, starting transfers between devices, shift(): lax.ppermute(value, 'tensor', [(s, (s + step) % count) for s in range(cou...  13.6 us
    pallas_call x1, Pallas kernels, right_second(): pl.pallas_call(functools.partial(right_second_kernel, len(messages)), in_...  10.7 us
    pallas_call x1, Pallas kernels, move(): pl.pallas_call(functools.partial(move_kernel, len(grads)), in_specs=[SMEM...  10.2 us
    pallas_call x1, Pallas kernels, descend(): pl.pallas_call(functools.partial(descend_kernel, len(grads), size), in_sp...  7.78 us
    pallas_call x1, Pallas kernels, right_first(): pl.pallas_call(functools.partial(right_first_kernel, len(grads)), in_spec...  7.13 us
    pallas_call x1, Pallas kernels, ortho_first(): pl.pallas_call(functools.partial(ortho_first_kernel, count), out_shape=[j...  6.45 us
  transfers between devices with their start and end apart: 18, of which 7 were waited for; matrix products, arithmetic and copies ran while one was open for 1% of the time, Pallas kernels for 22%

commit v1 on v0

v1 whole, which is shorter than its diff:
```python
import functools

import jax
import jax.numpy as jnp
from jax import lax
from jax.experimental import pallas as pl
from jax.experimental.pallas import tpu as pltpu
from jax.sharding import PartitionSpec as P


learn_rate = 0.1
momentum_decay = 0.9
older_share = learn_rate * (1.0 + momentum_decay)
bf16 = jnp.bfloat16
f32 = jnp.float32

VMEM = pl.BlockSpec(memory_space=pltpu.VMEM)
SMEM = pl.BlockSpec(memory_space=pltpu.SMEM)
HBM = pl.BlockSpec(memory_space=pltpu.HBM)
room = pltpu.CompilerParams(vmem_limit_bytes=28 * 2**20)


def dot(a, b, contract, precision=None):
    return lax.dot_general(
        a, b, (((contract[0],), (contract[1],)), ((), ())),
        precision=precision, preferred_element_type=f32,
    )


def exact(a, b, contract):
    return dot(a, b, contract, lax.Precision.HIGHEST)


def in_hbm(*values):
    return [pltpu.with_memory_space_constraint(v, pltpu.HBM) for v in values]


def loading(source, target, sems, size):
    copies = []
    for i in range(source.shape[0] // size):
        at = pl.ds(i * size, size)
        copies.append(pltpu.make_async_copy(source.at[at], target.at[at], sems.at[i]))
        copies[-1].start()
    return copies


def columns_of(place, width):
    return pl.ds(pl.multiple_of(place * width, width), width)


def write_pieces(out, parts, seen):
    at = 0
    for part in parts:
        out[:, at : at + part.shape[1]] = part
        at += part.shape[1]
    out[:, at:] = seen


def project_kernel(count, tokens, me_ref, f_hbm, h_hbm, w_hbm, kept, sent, w, h, f, total, sems):
    rank = kept.shape[0]
    span = w.shape[1] // count
    chunks = 4
    size = w.shape[0] // chunks
    first = pltpu.make_async_copy(f_hbm, f, sems.at[chunks])
    first.start()
    copies = []
    for i in range(chunks):
        at = pl.ds(i * size, size)
        copies.append(pltpu.make_async_copy(w_hbm.at[at], w.at[at], sems.at[i]))
        copies[-1].start()
    last = pltpu.make_async_copy(h_hbm, h, sems.at[chunks + 1])
    last.start()
    first.wait()
    for i in range(chunks):
        copies[i].wait()
        part = dot(f[:, i * size : (i + 1) * size], w[i * size : (i + 1) * size, :], (1, 0))
        total[...] = part if i == 0 else total[...] + part
    last.wait()
    both = dot(f[...], h[...], (1, 1)).astype(bf16)
    seen = jnp.concatenate(
        [both[:rank, :tokens], both[rank:, :tokens], both[rank:, tokens:]], 1
    )
    for out, start in ((kept, 0), (sent, 1)):
        parts = []
        for r in range(start, count, 2):
            part = total[:, columns_of(me_ref[0] ^ r, span)].astype(bf16)
            parts += [part[:rank], part[rank:]]
        write_pieces(out, parts, seen)


def project(me, factors, h, w, count, rank, tokens):
    _, depth = w.shape
    span = depth // count
    length = count * span + 3 * tokens
    message = jax.ShapeDtypeStruct((rank, length), bf16)
    return pl.pallas_call(
        functools.partial(project_kernel, count, tokens),
        in_specs=[SMEM, HBM, HBM, HBM],
        out_specs=[VMEM] * 2,
        out_shape=[message, message],
        scratch_shapes=[
            pltpu.VMEM(w.shape, bf16),
            pltpu.VMEM(h.shape, bf16),
            pltpu.VMEM(factors.shape, bf16),
            pltpu.VMEM((2 * rank, depth), f32),
            pltpu.SemaphoreType.DMA((6,)),
        ],
        compiler_params=room,
        name="project",
    )(me, *(pltpu.with_memory_space_constraint(x, pltpu.HBM) for x in (factors, h, w)))


def halve(kept, arrived, tokens, span):
    rank, length = kept.shape
    pieces = (length - 3 * tokens) // (2 * span)
    message = jax.ShapeDtypeStruct((rank, pieces * span + 3 * tokens), bf16)

    def kernel(kept, arrived, keep, send):
        total = (kept[...].astype(f32) + arrived[...].astype(f32)).astype(bf16)
        for out, start in ((keep, 0), (send, 1)):
            parts = [total[:, 2 * span * r : 2 * span * (r + 1)] for r in range(start, pieces, 2)]
            write_pieces(out, parts, total[:, 2 * span * pieces :])

    return pl.pallas_call(
        kernel, out_shape=[message] * 2, in_specs=[VMEM] * 2, out_specs=[VMEM] * 2,
        compiler_params=room, name="halve",
    )(kept, arrived)


def left_kernel(count, tokens, g_ref, *refs):
    messages, (mine, left) = refs[:count], refs[count:]
    span = g_ref.shape[1]
    total = messages[0][...].astype(f32)
    for k in range(1, count):
        total = total + messages[k][...].astype(f32)
    seen = total[:, 2 * span :].astype(bf16)
    older = dot(seen[:, tokens : 2 * tokens], g_ref[:tokens, :], (1, 0))
    mine[:, :span] = (
        total[:, :span] - learn_rate * dot(seen[:, :tokens], g_ref[:tokens, :], (1, 0))
    ).astype(bf16)
    later = total[:, span : 2 * span] - learn_rate * older
    mine[:, span:] = later.astype(bf16)
    left[...] = later - learn_rate * (
        momentum_decay * older + dot(seen[:, 2 * tokens :], g_ref[tokens:, :], (1, 0))
    )


def left_products(g, messages, tokens):
    rank, span = messages[0].shape[0], g.shape[1]
    return pl.pallas_call(
        functools.partial(left_kernel, len(messages), tokens),
        out_shape=[
            jax.ShapeDtypeStruct((rank, 2 * span), bf16),
            jax.ShapeDtypeStruct((rank, span), f32),
        ],
        in_specs=[VMEM] * (1 + len(messages)),
        out_specs=[VMEM] * 2,
        compiler_params=room,
        name="left",
    )(g, *messages)


def differ_kernel(mine, other, out):
    _, length = mine.shape
    span = length // 2
    diff = (mine[:, :span].astype(f32) - other[:, :span].astype(f32)).astype(bf16)
    both = (mine[:, span:].astype(f32) + other[:, span:].astype(f32)).astype(bf16)
    out[:, :span] = diff
    out[:, span:] = dot(both, diff, (1, 1)).astype(bf16)


def differ(mine, other):
    rank, length = mine.shape
    return pl.pallas_call(
        differ_kernel,
        out_shape=jax.ShapeDtypeStruct((rank, length // 2 + rank), bf16),
        in_specs=[VMEM] * 2,
        out_specs=VMEM,
        compiler_params=room,
        name="differ",
    )(mine, other)


def differ_later_kernel(mine, other, g_ref, out):
    span = mine.shape[1]
    diff = (mine[...].astype(f32) - other[...].astype(f32)).astype(bf16)
    out[:, :span] = diff
    out[:, span:] = dot(diff, g_ref[...], (1, 1)).astype(bf16)


def differ_later(mine, other, g):
    rank, span = mine.shape
    return pl.pallas_call(
        differ_later_kernel,
        out_shape=jax.ShapeDtypeStruct((rank, span + g.shape[0]), bf16),
        in_specs=[VMEM] * 3,
        out_specs=VMEM,
        compiler_params=room,
        name="differ_later",
    )(mine, other, g)


def inverse_factor(gram):
    size = gram.shape[0]
    high = 8
    tiles = [gram[high * t : high * (t + 1), :] for t in range(size // high)]
    columns = lax.broadcasted_iota(jnp.int32, (high, size), 1)
    rows = lax.broadcasted_iota(jnp.int32, (high, size), 0)
    scales = []
    for own in range(size // high):
        below = range(own, size // high)
        ahead = [
            {t: jnp.broadcast_to(tiles[t][:, k : k + 1], (high, size)) for t in below}
            for k in range(high * own, high * (own + 1))
        ]
        scale = jnp.ones((high, size), f32)
        for j in range(high):
            k = high * own + j
            pivot = ahead[j][own][j : j + 1, :]
            share = 1.0 / pivot
            row = jnp.where(columns[:1] == k, 1.0, tiles[own][j : j + 1, :]) * share
            later = [ahead[m][own][j : j + 1, :] * share for m in range(high)]
            for t in below:
                ratio = jnp.where(rows > j, ahead[j][t], 0.0) if t == own else ahead[j][t]
                drop = (columns == k) & (rows > j) if t == own else columns == k
                tiles[t] = jnp.where(drop, 0.0, tiles[t]) - ratio * row
                for m in range(j + 1, high):
                    ahead[m][t] = ahead[m][t] - ratio * later[m]
            scale = jnp.where(rows == j, pivot, scale)
        scales.append(scale)
    out = []
    for t in range(size // high):
        place = rows + high * t
        lower = jnp.where(place > columns, tiles[t], jnp.where(place == columns, 1.0, 0.0))
        out.append(lower * lax.rsqrt(scales[t]))
    return jnp.concatenate(out, 0)


def ortho_first_kernel(count, me_ref, left_ref, *refs):
    messages, (ortho, out, whole) = refs[:count], refs[count:]
    rank, span = left_ref.shape
    edge = jnp.zeros((rank, rank), f32)
    for k in range(count):
        place = me_ref[0] ^ k
        whole[:, columns_of(place, span)] = messages[k][:, :span]
        edge = edge + messages[k][:, span:].astype(f32)
    inverse = inverse_factor(dot(whole[...], whole[...], (1, 1)))
    near = exact(inverse, messages[0][:, :span].astype(f32), (1, 0)).astype(bf16)
    turned = exact(edge, inverse, (1, 1)).astype(bf16)
    out[...] = (left_ref[...] - 0.5 * dot(turned, near, (1, 0))).astype(bf16)
    ortho[...] = exact(inverse, whole[...].astype(f32), (1, 0)).astype(bf16)


def ortho_first(me, left, messages):
    count = len(messages)
    rank, span = left.shape
    return pl.pallas_call(
        functools.partial(ortho_first_kernel, count),
        out_shape=[
            jax.ShapeDtypeStruct((rank, span * count), bf16),
            jax.ShapeDtypeStruct((rank, span), bf16),
        ],
        in_specs=[SMEM] + [VMEM] * (1 + count),
        out_specs=[VMEM] * 2,
        scratch_shapes=[pltpu.VMEM((rank, span * count), bf16)],
        compiler_params=room,
        name="ortho_first",
    )(me, left, *messages)


def inverse_factor_loop(work, scales):
    size, width = work.shape
    high = 8
    columns = lax.broadcasted_iota(jnp.int32, (high, width), 1)
    rows = lax.broadcasted_iota(jnp.int32, (high, width), 0)

    def body(own, _):
        base = own * high
        tiles = [work[high * t : high * (t + 1), :] for t in range(size // high)]
        tiles.append(work[pl.ds(pl.multiple_of(base, high), high), :])
        starts = [high * t for t in range(size // high)] + [base]
        turned = [pltpu.roll(tile, width - base, 1) for tile in tiles]
        ahead = [
            [jnp.broadcast_to(tile[:, j : j + 1], (high, width)) for tile in turned]
            for j in range(high)
        ]
        scale = jnp.ones((high, width), f32)
        for j in range(high):
            pivot = ahead[j][-1][j : j + 1, :]
            share = 1.0 / pivot
            row = jnp.where(columns[:1] == base + j, 1.0, tiles[-1][j : j + 1, :]) * share
            later = [ahead[m][-1][j : j + 1, :] * share for m in range(high)]
            for t, start in enumerate(starts):
                below = rows > base + j - start
                ratio = jnp.where(below, ahead[j][t], 0.0)
                drop = (columns == base + j) & below
                tiles[t] = jnp.where(drop, 0.0, tiles[t]) - ratio * row
                for m in range(j + 1, high):
                    ahead[m][t] = ahead[m][t] - ratio * later[m]
            scale = jnp.where(rows == j, pivot, scale)
        for t in range(size // high):
            work[high * t : high * (t + 1), :] = tiles[t]
        scales[pl.ds(pl.multiple_of(base, high), high), :] = scale
        return 0

    lax.fori_loop(0, size // high, body, 0)
    across = lax.broadcasted_iota(jnp.int32, (size, size), 1)
    down = lax.broadcasted_iota(jnp.int32, (size, size), 0)
    lower = jnp.where(down > across, work[:, :size], jnp.where(down == across, 1.0, 0.0))
    return lower * lax.rsqrt(scales[:, :size])


def ortho_second_kernel(whole, ortho, inverse, work, scales):
    rank, depth = whole.shape
    work[...] = jnp.zeros_like(work)
    work[:, :rank] = dot(whole[...], whole[...], (1, 1))
    inverse[...] = inverse_factor_loop(work, scales)
    size = min(512, depth)

    def body(i, _):
        at = columns_of(i, size)
        ortho[:, at] = exact(inverse[...], whole[:, at].astype(f32), (1, 0)).astype(bf16)
        return 0

    lax.fori_loop(0, depth // size, body, 0)


def ortho_second(whole):
    rank = whole.shape[0]
    return pl.pallas_call(
        ortho_second_kernel,
        out_shape=[jax.ShapeDtypeStruct(whole.shape, bf16), jax.ShapeDtypeStruct((rank, rank), f32)],
        in_specs=[VMEM],
        out_specs=[VMEM] * 2,
        scratch_shapes=[pltpu.VMEM((rank, 2 * rank), f32)] * 2,
        compiler_params=room,
        name="ortho_second",
    )(whole)


def right_first_kernel(count, me_ref, ortho, h_hbm, w_hbm, *refs):
    grads, (out, h, w, h_sems, w_sems) = refs[:count], refs[count:]
    tokens, span = grads[0].shape
    half = w.shape[0] // 2
    (seeing,) = loading(h_hbm.at[pl.ds(0, tokens)], h, h_sems, tokens)
    copies = loading(w_hbm, w, w_sems, half)
    total = jnp.zeros((ortho.shape[0], tokens), f32)
    for k in range(count):
        total = total + dot(ortho[:, columns_of(me_ref[0] ^ k, span)], grads[k][...], (1, 1))
    seen = (learn_rate * total).astype(bf16)
    seeing.wait()
    for i in range(2):
        at = slice(i * half, (i + 1) * half)
        change = dot(seen, h[:, at], (1, 0))
        copies[i].wait()
        out[:, at] = (dot(ortho[...], w[at, :], (1, 1)) - change).astype(bf16)


def right_first(me, ortho, h, w, grads):
    return pl.pallas_call(
        functools.partial(right_first_kernel, len(grads)),
        in_specs=[SMEM, VMEM, HBM, HBM] + [VMEM] * len(grads),
        out_specs=VMEM,
        out_shape=jax.ShapeDtypeStruct((ortho.shape[0], w.shape[0]), bf16),
        scratch_shapes=[
            pltpu.VMEM((h.shape[0] // 2, h.shape[1]), bf16),
            pltpu.VMEM(w.shape, bf16),
            pltpu.SemaphoreType.DMA((1,)),
            pltpu.SemaphoreType.DMA((2,)),
        ],
        compiler_params=room,
        name="right_first",
    )(me, ortho, *in_hbm(h, w), *grads)


def turn_kernel(h, old, new):
    tokens = h.shape[0] // 2
    size = min(512, h.shape[1])
    for i in range(h.shape[1] // size):
        at = slice(i * size, (i + 1) * size)
        old[at, :] = (older_share * h[:tokens, at].astype(f32)).astype(bf16).T
        new[at, :] = (learn_rate * h[tokens:, at].astype(f32)).astype(bf16).T


def turn(h):
    tokens = h.shape[0] // 2
    return pl.pallas_call(
        turn_kernel,
        in_specs=[VMEM],
        out_specs=[VMEM] * 2,
        out_shape=[jax.ShapeDtypeStruct((h.shape[1], tokens), bf16)] * 2,
        compiler_params=room,
        name="turn",
    )(h)


def descend_kernel(count, size, me_ref, h_hbm, w_hbm, *refs):
    pieces, (out, h, u, grads, h_sems, loads, stores) = refs[:count], refs[count:]
    span = pieces[0].shape[1]
    blocks = u.shape[0] // size
    loading(h_hbm, h, h_sems, size)
    loading(w_hbm, u, loads, size)
    for k in range(count):
        grads[:, columns_of(me_ref[0] ^ k, span)] = pieces[k][...]

    def body(i, _):
        rows = pl.ds(pl.multiple_of(i * size, size), size)
        pltpu.make_async_copy(h_hbm.at[rows], h.at[rows], h_sems.at[i]).wait()
        change = dot(h[rows, :], grads[...], (1, 0))
        pltpu.make_async_copy(w_hbm.at[rows], u.at[rows], loads.at[i]).wait()
        u[rows, :] = (u[rows, :].astype(f32) - change).astype(bf16)
        pltpu.make_async_copy(u.at[rows], out.at[rows], stores.at[i]).start()
        return 0

    lax.fori_loop(0, blocks, body, 0)
    for i in range(blocks):
        at = pl.ds(i * size, size)
        pltpu.make_async_copy(u.at[at], out.at[at], stores.at[i]).wait()


def descend(me, turned, w, pieces):
    size = min(256, w.shape[0])
    blocks = w.shape[0] // size
    return pl.pallas_call(
        functools.partial(descend_kernel, len(pieces), size),
        in_specs=[SMEM, HBM, HBM] + [VMEM] * len(pieces),
        out_specs=HBM,
        out_shape=pltpu.HBM(w.shape, bf16),
        scratch_shapes=[
            pltpu.VMEM(turned.shape, bf16),
            pltpu.VMEM(w.shape, bf16),
            pltpu.VMEM((turned.shape[1], w.shape[1]), bf16),
            pltpu.SemaphoreType.DMA((blocks,)),
            pltpu.SemaphoreType.DMA((blocks,)),
            pltpu.SemaphoreType.DMA((blocks,)),
        ],
        compiler_params=room,
        name="descend",
    )(me, *in_hbm(turned, w), *pieces)


def descend_later_kernel(count, size, me_ref, h, u, *refs):
    pieces, (out, grads) = refs[:count], refs[count:]
    span = pieces[0].shape[1]
    for k in range(count):
        grads[:, columns_of(me_ref[0] ^ k, span)] = pieces[k][...]

    def body(i, _):
        rows = pl.ds(pl.multiple_of(i * size, size), size)
        out[rows, :] = (u[rows, :].astype(f32) - dot(h[rows, :], grads[...], (1, 0))).astype(bf16)
        return 0

    lax.fori_loop(0, u.shape[0] // size, body, 0)


def descend_later(me, turned, u, pieces):
    return pl.pallas_call(
        functools.partial(descend_later_kernel, len(pieces), min(256, u.shape[0])),
        in_specs=[SMEM] + [VMEM] * (2 + len(pieces)),
        out_specs=VMEM,
        out_shape=jax.ShapeDtypeStruct(u.shape, bf16),
        scratch_shapes=[pltpu.VMEM((turned.shape[1], u.shape[1]), bf16)],
        compiler_params=room,
        name="descend_later",
    )(me, turned, u, *pieces)


def right_second_kernel(count, me_ref, before, h_hbm, u_hbm, mine, other, *refs):
    messages, (out, whole, h, u, h_sems, sems) = refs[:count], refs[count:]
    rank, tokens = before.shape[0], h.shape[0]
    span = messages[0].shape[1] - tokens
    half = u.shape[0] // 2
    (seeing,) = loading(h_hbm.at[pl.ds(tokens, tokens)], h, h_sems, tokens)
    copies = loading(u_hbm, u, sems, half)
    newer = jnp.zeros((rank, tokens), f32)
    for k in range(count):
        whole[:, columns_of(me_ref[0] ^ k, span)] = messages[k][:, :span]
        newer = newer + messages[k][:, span:].astype(f32)
    newer = (learn_rate * newer).astype(bf16)
    turned = (0.5 * dot(whole[...], before[...], (1, 1))).astype(bf16)
    seeing.wait()
    for i in range(2):
        at = slice(i * half, (i + 1) * half)
        turn = (mine[:, at].astype(f32) - other[:, at].astype(f32)).astype(bf16)
        change = dot(turned, turn, (1, 0)) + dot(newer, h[:, at], (1, 0))
        copies[i].wait()
        out[:, at] = (dot(whole[...], u[at, :], (1, 1)) - change).astype(bf16)


def right_second(me, before, h, u, mine, other, messages):
    rank, depth = before.shape
    return pl.pallas_call(
        functools.partial(right_second_kernel, len(messages)),
        in_specs=[SMEM, VMEM, HBM, HBM] + [VMEM] * (2 + len(messages)),
        out_specs=[VMEM] * 2,
        out_shape=[
            jax.ShapeDtypeStruct((rank, u.shape[0]), bf16),
            jax.ShapeDtypeStruct((rank, depth), bf16),
        ],
        scratch_shapes=[
            pltpu.VMEM((h.shape[0] // 2, h.shape[1]), bf16),
            pltpu.VMEM(u.shape, bf16),
            pltpu.SemaphoreType.DMA((1,)),
            pltpu.SemaphoreType.DMA((2,)),
        ],
        compiler_params=room,
        name="right_second",
    )(me, before, *in_hbm(h, u), mine, other, *messages)


def move_kernel(first, second, inverse, u, a0, b0, a1, b1, out, turned, ortho, block, stores):
    rank = first.shape[0]
    size = min(512, u.shape[0])
    both = jnp.concatenate(
        [
            a0[...].astype(f32) - b0[...].astype(f32),
            exact(inverse[...], a1[...].astype(f32) - b1[...].astype(f32), (1, 0)),
        ],
        0,
    )
    turned[...] = (0.5 * both).astype(bf16).T
    ortho[:rank, :] = first[...]
    ortho[rank:, :] = second[...]

    def body(i, _):
        rows = pl.ds(pl.multiple_of(i * size, size), size)
        block[rows, :] = (
            u[rows, :].astype(f32) - dot(turned[rows, :], ortho[...], (1, 0))
        ).astype(bf16)
        pltpu.make_async_copy(block.at[rows], out.at[rows], stores.at[i]).start()
        return 0

    blocks = u.shape[0] // size
    lax.fori_loop(0, blocks, body, 0)
    for i in range(blocks):
        at = pl.ds(i * size, size)
        pltpu.make_async_copy(block.at[at], out.at[at], stores.at[i]).wait()


def move(first, second, inverse, u, pairs):
    rank = first.shape[0]
    blocks = u.shape[0] // min(512, u.shape[0])
    return pl.pallas_call(
        move_kernel,
        in_specs=[VMEM] * 8,
        out_specs=HBM,
        out_shape=pltpu.HBM(u.shape, bf16),
        scratch_shapes=[
            pltpu.VMEM((u.shape[0], 2 * rank), bf16),
            pltpu.VMEM((2 * rank, u.shape[1]), bf16),
            pltpu.VMEM(u.shape, bf16),
            pltpu.SemaphoreType.DMA((blocks,)),
        ],
        compiler_params=room,
        name="move",
    )(first, second, inverse, u, *pairs)


def swap(value, which, beside=None, then=lambda arrived, extra: arrived):
    count = lax.axis_size("replica")

    def branch(x, mask):
        arrived = lax.ppermute(x, "replica", [(s, s ^ mask) for s in range(count)])
        return then(arrived, beside() if beside else None)

    branches = [functools.partial(branch, mask=mask) for mask in range(1, count)]
    return lax.switch(which - 1, branches, value)


def across(value, bit):
    count = lax.axis_size("tensor")
    return lax.ppermute(value, "tensor", [(s, s ^ bit) for s in range(count)])


def spread(value):
    pieces = [value]
    for r in range(1, lax.axis_size("tensor")):
        low = r & -r
        pieces.append(across(pieces[r ^ low], low))
    return pieces


def after(value, *events):
    return lax.optimization_barrier((value, *events))[0]


def per_device(weights, hidden, out_grad, factor_start, matching):
    return both_steps(weights[0], hidden[0], out_grad[0], factor_start, matching)[None]


def both_steps(w, h, g, factor_start, matching):
    count = lax.axis_size("tensor")
    me = lax.axis_index("tensor").astype(jnp.int32).reshape(1)
    steps, rank, width = factor_start.shape
    tokens = g.shape[0] // steps
    span = g.shape[1]
    olds, news = {0: g[:tokens]}, {0: g[tokens:]}

    def gather(pieces, event, *indices):
        for r in indices:
            low = r & -r
            pieces[r] = across(after(pieces[r ^ low], event), low)

    odd = range(1, count, 2)
    even = range(2, count, 2)
    kept, sent = project(me, factor_start.reshape(steps * rank, width), h, w, count, rank, tokens)
    bit = 1
    while True:
        arrived = across(sent, bit)
        if bit == 1:
            old_turned, new_turned = turn(after(h, sent))
            gather(olds, arrived, 1)
        bit *= 2
        if bit == count:
            break
        kept, sent = halve(kept, arrived, tokens, span)
    mine, left = left_products(g, [kept, arrived], tokens)
    gather(olds, mine, *even)
    other = swap(mine, matching[0])
    message = differ(mine, other)
    messages = spread(message)
    ortho0, left = ortho_first(me, left, messages)
    gather(olds, left, *odd[1:])
    other = swap(left, matching[1])
    message = differ_later(left, other, news[0])
    pieces = spread(message)
    olds = [olds[r] for r in range(count)]
    right0 = right_first(me, after(ortho0, message), h, w, olds)
    gather(news, pieces[2], *even)
    gather(news, pieces[2], 1)
    other0, u = swap(
        after(right0, pieces[2]),
        matching[0],
        lambda: descend(me, old_turned, w, olds),
        lambda *both: both,
    )
    gather(news, other0, *odd[1:])
    right1, whole = right_second(me, ortho0, h, u, right0, other0, pieces)
    news = [news[r] for r in range(count)]

    other1, (second, u) = swap(
        right1,
        matching[1],
        lambda: (ortho_second(whole), descend_later(me, new_turned, u, news)),
        lambda *both: both,
    )
    return move(ortho0, *second, u, (right0, other0, right1, other1))


def solution(mesh):
    return jax.shard_map(
        per_device,
        mesh=mesh,
        in_specs=(
            P("replica", "tensor", None),
            P("replica", None, "tensor"),
            P("replica", None, "tensor"),
            P(None, None, "tensor"),
            P(),
        ),
        out_specs=P("replica", "tensor", None),
        check_vma=False,
    )
```

time: 131 us -> 132 us (level)
  the two profiles are of different devices: /device:TPU:1 before, /device:TPU:0 now
where the time goes in v1:
time: 132 us
  waiting for transfers between devices  57.9 us (44%)
  Pallas kernels  46.4 us (35%)
  starting transfers between devices  24.5 us (19%)
  between operations  1.66 us (1%)
  local copies, waits for them, and re-layouts  1.36 us (1%)
    ppermute x14, waiting for transfers between devices, across(): return lax.ppermute(value, 'tensor', [(s, s ^ bit) for s in range(count)])  46.6 us
    ppermute x14, starting transfers between devices, across(): return lax.ppermute(value, 'tensor', [(s, s ^ bit) for s in range(count)])  21.6 us
    ppermute x4, waiting for transfers between devices, branch(): arrived = lax.ppermute(x, 'replica', [(s, s ^ mask) for s in range(count)])  11.3 us
    pallas_call x1, Pallas kernels, descend(): pl.pallas_call(functools.partial(descend_kernel, len(pieces), size), in_s...  7.06 us
    pallas_call x1, Pallas kernels, right_second(): pl.pallas_call(functools.partial(right_second_kernel, len(messages)), in_...  6.53 us
    pallas_call x1, Pallas kernels, right_first(): pl.pallas_call(functools.partial(right_first_kernel, len(grads)), in_spec...  6.3 us
    pallas_call x1, Pallas kernels, move(): pl.pallas_call(move_kernel, in_specs=[VMEM] * 8, out_specs=HBM, out_shape...  5.93 us
    pallas_call x1, Pallas kernels, project(): pl.pallas_call(functools.partial(project_kernel, count, tokens), in_specs...  5.28 us
  transfers between devices with their start and end apart: 18, of which 12 were waited for; matrix products, arithmetic and copies ran while one was open for 1% of the time, Pallas kernels for 26%

profile of v1, /device:TPU:0, one launch (start us, length us, event | category | flops | bytes accessed | tf_op | source)
XLA Modules:
  0.0 132.1 jit_solution(12133001055124573633)
XLA Ops:
  0.0 5.3 %project.1 = (bf16[64,2816]{1,0:T(8,128)(2,1)S(1)}, bf16[64,2816]{1,0:T(8,128)(2,1)S(1)}) custom-call(s32[1]{0:T(128)} %bitcast.me_ref, bf16[128,2048]{1,0:T(8,128)(2,1)} %bitcast.26, bf16[512,2048]{1,0:T(8,128)(2,1)} %bitcast.12, bf16[2048,2048]{1,0:T(8,128)(2,1)} %bitcast.17), custom_call_target="tpu_custom_call" | custom-call | tf_op jit(solution)/shard_map/project/pallas_call | solution.py:96
  5.3 3.1 %collective-permute-start.28 = (bf16[64,2816]{1,0:T(8,128)(2,1)S(1)}, bf16[64,2816]{1,0:T(8,128)(2,1)S(1)}, u32[]{:S(2)}, u32[]{:S(2)}) collective-permute-start(bf16[64,2816]{1,0:T(8,128)(2,1)S(1)} %get-tuple-element.433), channel_id=1, source_target_pairs={{0,1},{1,0},{2,3},{3,2},{4,5},{5,4},{6,7},{7,6},{8,9},{9,8},{10,11... | collective-permute-start | bytes 1081352 | tf_op jit(solution)/shard_map/ppermute | solution.py:572
  8.4 8.4 %collective-permute-done.28.arrived = bf16[64,2816]{1,0:T(8,128)(2,1)S(1)} collective-permute-done((bf16[64,2816]{1,0:T(8,128)(2,1)S(1)}, bf16[64,2816]{1,0:T(8,128)(2,1)S(1)}, u32[]{:S(2)}, u32[]{:S(2)}) %collective-permute-start.28) | collective-permute-done | bytes 360480 | tf_op jit(solution)/shard_map/ppermute | solution.py:572
  16.9 2.8 %collective-permute-start.29 = (bf16[64,1792]{1,0:T(8,128)(2,1)S(1)}, bf16[64,1792]{1,0:T(8,128)(2,1)S(1)}, u32[]{:S(2)}, u32[]{:S(2)}) collective-permute-start(bf16[64,1792]{1,0:T(8,128)(2,1)S(1)} %get-tuple-element.435), channel_id=1, source_target_pairs={{0,2},{1,3},{2,0},{3,1},{4,6},{5,7},{6,4},{7,5},{8,10},{9,11},{10,... | collective-permute-start | bytes 688136 | tf_op jit(solution)/shard_map/ppermute | solution.py:572
  20.5 9.1 %collective-permute-done.29.refs_1_ = bf16[64,1792]{1,0:T(8,128)(2,1)S(1)} collective-permute-done((bf16[64,1792]{1,0:T(8,128)(2,1)S(1)}, bf16[64,1792]{1,0:T(8,128)(2,1)S(1)}, u32[]{:S(2)}, u32[]{:S(2)}) %collective-permute-start.29) | collective-permute-done | bytes 229408 | tf_op jit(solution)/shard_map/ppermute | solution.py:572
  31.2 6.9 %conditional.4 = (bf16[64,1024]{1,0:T(8,128)(2,1)}) conditional(s32[]{:T(128)} %bitcast.5, bf16[64,1024]{1,0:T(8,128)(2,1)S(1)} %get-tuple-element.437.mine, bf16[64,1024]{1,0:T(8,128)(2,1)S(1)} %get-tuple-element.437.mine, bf16[64,1024]{1,0:T(8,128)(2,1)S(1)} %get-tuple-element.437.mine, ...), branch_computations={%region_0.0_spmd, %region_1.0_spmd, %region_2.0_spmd, %region_3.0_... | conditional | bytes 524336 | solution.py:567
  32.2 5.9 %collective-permute-done.6 = bf16[64,1024]{1,0:T(8,128)(2,1)} collective-permute-done((bf16[64,1024]{1,0:T(8,128)(2,1)S(1)}, bf16[64,1024]{1,0:T(8,128)(2,1)}, u32[]{:S(2)}, u32[]{:S(2)}) %collective-permute-start.6) | collective-permute-done | bytes 131104 | tf_op jit(solution)/shard_map/cond/branch_6_fun/ppermute | solution.py:563
  39.2 3.0 %collective-permute-start.31 = (bf16[64,576]{1,0:T(8,128)(2,1)S(1)}, bf16[64,576]{1,0:T(8,128)(2,1)S(1)}, u32[]{:S(2)}, u32[]{:S(2)}) collective-permute-start(bf16[64,576]{1,0:T(8,128)(2,1)S(1)} %differ.1.refs_0_), channel_id=1, source_target_pairs={{0,2},{1,3},{2,0},{3,1},{4,6},{5,7},{6,4},{7,5},{8,10},{9,11},{10,... | collective-permute-start | bytes 221192 | tf_op jit(solution)/shard_map/ppermute | solution.py:572
  43.1 2.5 %collective-permute-done.31.refs_2_ = bf16[64,576]{1,0:T(8,128)(2,1)S(1)} collective-permute-done((bf16[64,576]{1,0:T(8,128)(2,1)S(1)}, bf16[64,576]{1,0:T(8,128)(2,1)S(1)}, u32[]{:S(2)}, u32[]{:S(2)}) %collective-permute-start.31) | collective-permute-done | bytes 73760 | tf_op jit(solution)/shard_map/ppermute | solution.py:572
  45.6 3.7 %collective-permute-start.32 = (bf16[64,576]{1,0:T(8,128)(2,1)S(1)}, bf16[64,576]{1,0:T(8,128)(2,1)S(1)}, u32[]{:S(2)}, u32[]{:S(2)}) collective-permute-start(bf16[64,576]{1,0:T(8,128)(2,1)S(1)} %collective-permute-done.31.refs_2_), channel_id=1, source_target_pairs={{0,1},{1,0},{2,3},{3,2},{4,5},{5,4},{6,7},{7,6},{8,9},{9,8},{10,11... | collective-permute-start | bytes 221192 | tf_op jit(solution)/shard_map/ppermute | solution.py:572
  49.9 1.8 %collective-permute-done.32.refs_3_ = bf16[64,576]{1,0:T(8,128)(2,1)S(1)} collective-permute-done((bf16[64,576]{1,0:T(8,128)(2,1)S(1)}, bf16[64,576]{1,0:T(8,128)(2,1)S(1)}, u32[]{:S(2)}, u32[]{:S(2)}) %collective-permute-start.32) | collective-permute-done | bytes 73760 | tf_op jit(solution)/shard_map/ppermute | solution.py:572
  51.7 2.6 %ortho_first.1 = (bf16[64,2048]{1,0:T(8,128)(2,1)S(1)}, bf16[64,512]{1,0:T(8,128)(2,1)S(1)}) custom-call(s32[1]{0:T(128)} %bitcast.me_ref, f32[64,512]{1,0:T(8,128)S(1)} %get-tuple-element.436.left_ref, bf16[64,576]{1,0:T(8,128)(2,1)S(1)} %differ.1.refs_0_, bf16[64,576]{1,0:T(8,128)(2,1)S(1)} %collective-permute-done.30.refs_1_, ...), custom_call_target="tpu_custom_call" | custom-call | tf_op jit(solution)/shard_map/ortho_first/pallas_call | solution.py:257
  54.3 4.5 %conditional.5 = (bf16[64,512]{1,0:T(8,128)(2,1)}) conditional(s32[]{:T(128)} %bitcast.6, bf16[64,512]{1,0:T(8,128)(2,1)S(1)} %get-tuple-element.439.mine, bf16[64,512]{1,0:T(8,128)(2,1)S(1)} %get-tuple-element.439.mine, bf16[64,512]{1,0:T(8,128)(2,1)S(1)} %get-tuple-element.439.mine, ...), branch_computations={%region_7.0_spmd, %region_8.0_spmd, %region_9.0_spmd, %region_10.0... | conditional | bytes 262192 | solution.py:567
  54.3 1.5 %collective-permute-start.10 = (bf16[64,512]{1,0:T(8,128)(2,1)S(1)}, bf16[64,512]{1,0:T(8,128)(2,1)}, u32[]{:S(2)}, u32[]{:S(2)}) collective-permute-start(bf16[64,512]{1,0:T(8,128)(2,1)S(1)} %param.10), channel_id=1, source_target_pairs={{0,16},{4,20},{8,24},{12,28},{16,0},{20,4},{24,8},{28,12},{1,17},{... | collective-permute-start | bytes 196616 | tf_op jit(solution)/shard_map/cond/branch_3_fun/ppermute | solution.py:563
  55.9 2.9 %collective-permute-done.10 = bf16[64,512]{1,0:T(8,128)(2,1)} collective-permute-done((bf16[64,512]{1,0:T(8,128)(2,1)S(1)}, bf16[64,512]{1,0:T(8,128)(2,1)}, u32[]{:S(2)}, u32[]{:S(2)}) %collective-permute-start.10) | collective-permute-done | bytes 65568 | tf_op jit(solution)/shard_map/cond/branch_3_fun/ppermute | solution.py:563
  61.3 2.0 %collective-permute-start.33 = (bf16[256,512]{1,0:T(8,128)(2,1)S(1)}, bf16[256,512]{1,0:T(8,128)(2,1)S(1)}, u32[]{:S(2)}, u32[]{:S(2)}) collective-permute-start(bf16[256,512]{1,0:T(8,128)(2,1)S(1)} %get-tuple-element.442.refs_0_), channel_id=1, source_target_pairs={{0,1},{1,0},{2,3},{3,2},{4,5},{5,4},{6,7},{7,6},{8,9},{9,8},{10,11... | collective-permute-start | bytes 786440 | tf_op jit(solution)/shard_map/ppermute | solution.py:572
  63.4 4.0 %collective-permute-done.36.refs_2_ = bf16[64,768]{1,0:T(8,128)(2,1)S(1)} collective-permute-done((bf16[64,768]{1,0:T(8,128)(2,1)S(1)}, bf16[64,768]{1,0:T(8,128)(2,1)S(1)}, u32[]{:S(2)}, u32[]{:S(2)}) %collective-permute-start.36) | collective-permute-done | bytes 98336 | tf_op jit(solution)/shard_map/ppermute | solution.py:572
  67.9 1.9 %turn.1 = (bf16[2048,256]{1,0:T(8,128)(2,1)}, bf16[2048,256]{1,0:T(8,128)(2,1)}) custom-call(bf16[512,2048]{1,0:T(8,128)(2,1)S(1)} %bitcast.15), custom_call_target="tpu_custom_call" | custom-call | tf_op jit(solution)/shard_map/turn/pallas_call | solution.py:387
  69.8 1.8 %collective-permute-start.39 = (bf16[256,512]{1,0:T(8,128)(2,1)}, bf16[256,512]{1,0:T(8,128)(2,1)S(1)}, u32[]{:S(2)}, u32[]{:S(2)}) collective-permute-start(bf16[256,512]{1,0:T(8,128)(2,1)} %get-tuple-element.452.g_ref), channel_id=1, source_target_pairs={{0,1},{1,0},{2,3},{3,2},{4,5},{5,4},{6,7},{7,6},{8,9},{9,8},{10,11... | collective-permute-start | bytes 786440 | tf_op jit(solution)/shard_map/ppermute | solution.py:572
  71.6 5.3 %collective-permute-done.33.refs_1_ = bf16[256,512]{1,0:T(8,128)(2,1)S(1)} collective-permute-done((bf16[256,512]{1,0:T(8,128)(2,1)S(1)}, bf16[256,512]{1,0:T(8,128)(2,1)S(1)}, u32[]{:S(2)}, u32[]{:S(2)}) %collective-permute-start.33) | collective-permute-done | bytes 262176 | tf_op jit(solution)/shard_map/ppermute | solution.py:572
  76.9 5.1 %collective-permute-done.35.refs_3_ = bf16[256,512]{1,0:T(8,128)(2,1)S(1)} collective-permute-done((bf16[256,512]{1,0:T(8,128)(2,1)S(1)}, bf16[256,512]{1,0:T(8,128)(2,1)S(1)}, u32[]{:S(2)}, u32[]{:S(2)}) %collective-permute-start.35) | collective-permute-done | bytes 262176 | tf_op jit(solution)/shard_map/ppermute | solution.py:572
  82.0 6.3 %right_first.1.mine.a0 = bf16[64,2048]{1,0:T(8,128)(2,1)} custom-call(s32[1]{0:T(128)} %bitcast.me_ref, bf16[64,2048]{1,0:T(8,128)(2,1)S(1)} %get-tuple-element.440.ortho.before.first, bf16[512,2048]{1,0:T(8,128)(2,1)} %bitcast.13, bf16[2048,2048]{1,0:T(8,128)(2,1)} %bitcast.18, bf16[256,512]{1,0:T(8,128)(2,1)S(1)} %get-tuple-element.442.refs_0_, ...), custom_call_target="tpu_custom_call" | custom-call | tf_op jit(solution)/shard_map/right_first/pallas_call | solution.py:360
  88.3 9.8 %conditional.6 = (bf16[64,2048]{1,0:T(8,128)(2,1)}, bf16[2048,2048]{1,0:T(8,128)(2,1)}) conditional(s32[]{:T(128)} %bitcast.5, (bf16[64,2048]{1,0:T(8,128)(2,1)}, s32[1]{0:T(128)}, bf16[2048,256]{1,0:T(8,128)(2,1)}, bf16[2048,2048]{1,0:T(8,128)(2,1)}, bf16[256,512]{1,0:T(8,128)(2,1)S(1)}, ...), branch_computations={%region_14.0_spmd, %region_15.0_spmd, %region_16.0_spmd, %region_1... | conditional | bytes 1048632 | solution.py:567
  88.4 7.1 %descend.13 = bf16[2048,2048]{1,0:T(8,128)(2,1)} custom-call(s32[1]{0:T(128)} %get-tuple-element.322.me_ref, bf16[2048,256]{1,0:T(8,128)(2,1)} %get-tuple-element.323.h_hbm, bf16[2048,2048]{1,0:T(8,128)(2,1)} %get-tuple-element.324.w_hbm, bf16[256,512]{1,0:T(8,128)(2,1)S(1)} %get-tuple-element.325.refs_0_, bf16[256,512]{1,0:T(8,128)(2,1)S(1)} %get-tuple-element.326.refs_1_, ...), custom_call_target="tpu_custom_call" | custom-call | tf_op jit(solution)/shard_map/cond/branch_6_fun/descend/pallas_call | solution.py:424
  95.5 2.6 %collective-permute-done.20 = bf16[64,2048]{1,0:T(8,128)(2,1)} collective-permute-done((bf16[64,2048]{1,0:T(8,128)(2,1)}, bf16[64,2048]{1,0:T(8,128)(2,1)}, u32[]{:S(2)}, u32[]{:S(2)}) %collective-permute-start.20) | collective-permute-done | bytes 262176 | tf_op jit(solution)/shard_map/cond/branch_6_fun/ppermute | solution.py:563
  98.2 2.0 %collective-permute-start.37 = (bf16[64,768]{1,0:T(8,128)(2,1)S(1)}, bf16[64,768]{1,0:T(8,128)(2,1)S(1)}, u32[]{:S(2)}, u32[]{:S(2)}) collective-permute-start(bf16[64,768]{1,0:T(8,128)(2,1)S(1)} %differ_later.1.refs_0_), channel_id=1, source_target_pairs={{0,1},{1,0},{2,3},{3,2},{4,5},{5,4},{6,7},{7,6},{8,9},{9,8},{10,11... | collective-permute-start | bytes 294920 | tf_op jit(solution)/shard_map/ppermute | solution.py:572
  100.3 9.4 %collective-permute-done.37.refs_1_ = bf16[64,768]{1,0:T(8,128)(2,1)S(1)} collective-permute-done((bf16[64,768]{1,0:T(8,128)(2,1)S(1)}, bf16[64,768]{1,0:T(8,128)(2,1)S(1)}, u32[]{:S(2)}, u32[]{:S(2)}) %collective-permute-start.37) | collective-permute-done | bytes 98336 | tf_op jit(solution)/shard_map/ppermute | solution.py:572
  110.8 6.5 %right_second.1 = (bf16[64,2048]{1,0:T(8,128)(2,1)S(1)}, bf16[64,2048]{1,0:T(8,128)(2,1)S(1)}) custom-call(s32[1]{0:T(128)} %bitcast.me_ref, bf16[64,2048]{1,0:T(8,128)(2,1)S(1)} %get-tuple-element.440.ortho.before.first, bf16[512,2048]{1,0:T(8,128)(2,1)} %bitcast.14, bf16[2048,2048]{1,0:T(8,128)(2,1)} %get-tuple-element.447.u_hbm, ...), custom_call_target="tpu_custom_call" | custom-call | tf_op jit(solution)/shard_map/right_second/pallas_call | solution.py:492
  117.4 8.6 %conditional.7 = (bf16[64,2048]{1,0:T(8,128)(2,1)}, bf16[64,2048]{1,0:T(8,128)(2,1)S(1)}, f32[64,64]{1,0:T(8,128)S(1)}, bf16[2048,2048]{1,0:T(8,128)(2,1)S(1)}) conditional(s32[]{:T(128)} %bitcast.6, (bf16[64,2048]{1,0:T(8,128)(2,1)S(1)}, bf16[64,2048]{1,0:T(8,128)(2,1)S(1)}, s32[1]{0:T(128)}, ...), branch_computations={%region_21.0_spmd, %region_22.0_spmd, %region_23.0_spmd, %region_2... | conditional | bytes 1048648 | solution.py:567
  117.7 3.7 %ortho_second.10 = (bf16[64,2048]{1,0:T(8,128)(2,1)S(1)}, f32[64,64]{1,0:T(8,128)S(1)}) custom-call(bf16[64,2048]{1,0:T(8,128)(2,1)S(1)} %get-tuple-element.363.whole), custom_call_target="tpu_custom_call" | custom-call | tf_op jit(solution)/shard_map/cond/branch_3_fun/ortho_second/pallas_call | solution.py:330
  121.4 4.6 %descend_later.10 = bf16[2048,2048]{1,0:T(8,128)(2,1)S(1)} custom-call(s32[1]{0:T(128)} %get-tuple-element.366.me_ref, bf16[2048,256]{1,0:T(8,128)(2,1)S(1)} %get-tuple-element.367.h, bf16[2048,2048]{1,0:T(8,128)(2,1)S(1)} %get-tuple-element.368.u, bf16[256,512]{1,0:T(8,128)(2,1)S(1)} %get-tuple-element.369.refs_0_, ...), custom_call_target="tpu_custom_call" | custom-call | tf_op jit(solution)/shard_map/cond/branch_3_fun/descend_later/pallas_call | solution.py:457
  126.0 5.9 %move.1 = bf16[2048,2048]{1,0:T(8,128)(2,1)} custom-call(bf16[64,2048]{1,0:T(8,128)(2,1)S(1)} %get-tuple-element.440.ortho.before.first, bf16[64,2048]{1,0:T(8,128)(2,1)S(1)} %get-tuple-element.454.second, f32[64,64]{1,0:T(8,128)S(1)} %get-tuple-element.455.inverse, bf16[2048,2048]{1,0:T(8,128)(2,1)S(1)} %get-tuple-element.456.u, ...), custom_call_target="tpu_custom_call" | custom-call | tf_op jit(solution)/shard_map/move/pallas_call | solution.py:543
  (35 shorter events, 9.6 us)
Async XLA Ops:
  0.0 67.9 %copy-start = (bf16[1,512,2048]{2,1,0:T(8,128)(2,1)S(1)}, bf16[1,512,2048]{2,1,0:T(8,128)(2,1)}, u32[]{:S(2)}) copy-start(bf16[1,512,2048]{2,1,0:T(8,128)(2,1)} %param.34) | copy-start | bytes 6291460
  0.0 19.7 %copy-start.1 = (bf16[1,512,512]{2,1,0:T(8,128)(2,1)S(1)}, bf16[1,512,512]{2,1,0:T(8,128)(2,1)}, u32[]{:S(2)}) copy-start(bf16[1,512,512]{2,1,0:T(8,128)(2,1)} %param.35) | copy-start | bytes 1572868
  0.0 29.9 %copy-start.5 = (s32[2]{0:T(128)S(1)}, s32[2]{0:T(128)}, u32[]{:S(2)}) copy-start(s32[2]{0:T(128)} %param.37) | copy-start | bytes 28
  5.3 11.5 %collective-permute-start.28 = (bf16[64,2816]{1,0:T(8,128)(2,1)S(1)}, bf16[64,2816]{1,0:T(8,128)(2,1)S(1)}, u32[]{:S(2)}, u32[]{:S(2)}) collective-permute-start(bf16[64,2816]{1,0:T(8,128)(2,1)S(1)} %get-tuple-element.433), channel_id=1, source_target_pairs={{0,1},{1,0},{2,3},{3,2},{4,5},{5,4},{6,7},{7,6},{8,9},{9,8},{10,11... | collective-permute-start | bytes 1081352 | tf_op jit(solution)/shard_map/ppermute | solution.py:572
  16.9 12.6 %collective-permute-start.29 = (bf16[64,1792]{1,0:T(8,128)(2,1)S(1)}, bf16[64,1792]{1,0:T(8,128)(2,1)S(1)}, u32[]{:S(2)}, u32[]{:S(2)}) collective-permute-start(bf16[64,1792]{1,0:T(8,128)(2,1)S(1)} %get-tuple-element.435), channel_id=1, source_target_pairs={{0,2},{1,3},{2,0},{3,1},{4,6},{5,7},{6,4},{7,5},{8,10},{9,11},{10,... | collective-permute-start | bytes 688136 | tf_op jit(solution)/shard_map/ppermute | solution.py:572
  29.8 33.5 %collective-permute-start.34 = (bf16[256,512]{1,0:T(8,128)(2,1)S(1)}, bf16[256,512]{1,0:T(8,128)(2,1)S(1)}, u32[]{:S(2)}, u32[]{:S(2)}) collective-permute-start(bf16[256,512]{1,0:T(8,128)(2,1)S(1)} %get-tuple-element.442.refs_0_), channel_id=1, source_target_pairs={{0,2},{1,3},{2,0},{3,1},{4,6},{5,7},{6,4},{7,5},{8,10},{9,11},{10,... | collective-permute-start | bytes 786440 | tf_op jit(solution)/shard_map/ppermute | solution.py:572
  31.2 6.9 %collective-permute-start.6 = (bf16[64,1024]{1,0:T(8,128)(2,1)S(1)}, bf16[64,1024]{1,0:T(8,128)(2,1)}, u32[]{:S(2)}, u32[]{:S(2)}) collective-permute-start(bf16[64,1024]{1,0:T(8,128)(2,1)S(1)} %param.6), channel_id=1, source_target_pairs={{0,28},{4,24},{8,20},{12,16},{16,12},{20,8},{24,4},{28,0},{1,29},{... | collective-permute-start | bytes 393224 | tf_op jit(solution)/shard_map/cond/branch_6_fun/ppermute | solution.py:563
  39.2 6.4 %collective-permute-start.31 = (bf16[64,576]{1,0:T(8,128)(2,1)S(1)}, bf16[64,576]{1,0:T(8,128)(2,1)S(1)}, u32[]{:S(2)}, u32[]{:S(2)}) collective-permute-start(bf16[64,576]{1,0:T(8,128)(2,1)S(1)} %differ.1.refs_0_), channel_id=1, source_target_pairs={{0,2},{1,3},{2,0},{3,1},{4,6},{5,7},{6,4},{7,5},{8,10},{9,11},{10,... | collective-permute-start | bytes 221192 | tf_op jit(solution)/shard_map/ppermute | solution.py:572
  42.1 7.8 %collective-permute-start.30 = (bf16[64,576]{1,0:T(8,128)(2,1)S(1)}, bf16[64,576]{1,0:T(8,128)(2,1)S(1)}, u32[]{:S(2)}, u32[]{:S(2)}) collective-permute-start(bf16[64,576]{1,0:T(8,128)(2,1)S(1)} %differ.1.refs_0_), channel_id=1, source_target_pairs={{0,1},{1,0},{2,3},{3,2},{4,5},{5,4},{6,7},{7,6},{8,9},{9,8},{10,11... | collective-permute-start | bytes 221192 | tf_op jit(solution)/shard_map/ppermute | solution.py:572
  45.6 6.1 %collective-permute-start.32 = (bf16[64,576]{1,0:T(8,128)(2,1)S(1)}, bf16[64,576]{1,0:T(8,128)(2,1)S(1)}, u32[]{:S(2)}, u32[]{:S(2)}) collective-permute-start(bf16[64,576]{1,0:T(8,128)(2,1)S(1)} %collective-permute-done.31.refs_2_), channel_id=1, source_target_pairs={{0,1},{1,0},{2,3},{3,2},{4,5},{5,4},{6,7},{7,6},{8,9},{9,8},{10,11... | collective-permute-start | bytes 221192 | tf_op jit(solution)/shard_map/ppermute | solution.py:572
  54.3 4.4 %collective-permute-start.10 = (bf16[64,512]{1,0:T(8,128)(2,1)S(1)}, bf16[64,512]{1,0:T(8,128)(2,1)}, u32[]{:S(2)}, u32[]{:S(2)}) collective-permute-start(bf16[64,512]{1,0:T(8,128)(2,1)S(1)} %param.10), channel_id=1, source_target_pairs={{0,16},{4,20},{8,24},{12,28},{16,0},{20,4},{24,8},{28,12},{1,17},{... | collective-permute-start | bytes 196616 | tf_op jit(solution)/shard_map/cond/branch_3_fun/ppermute | solution.py:563
  59.9 7.4 %collective-permute-start.36 = (bf16[64,768]{1,0:T(8,128)(2,1)S(1)}, bf16[64,768]{1,0:T(8,128)(2,1)S(1)}, u32[]{:S(2)}, u32[]{:S(2)}) collective-permute-start(bf16[64,768]{1,0:T(8,128)(2,1)S(1)} %differ_later.1.refs_0_), channel_id=1, source_target_pairs={{0,2},{1,3},{2,0},{3,1},{4,6},{5,7},{6,4},{7,5},{8,10},{9,11},{10,... | collective-permute-start | bytes 294920 | tf_op jit(solution)/shard_map/ppermute | solution.py:572
  61.3 15.6 %collective-permute-start.33 = (bf16[256,512]{1,0:T(8,128)(2,1)S(1)}, bf16[256,512]{1,0:T(8,128)(2,1)S(1)}, u32[]{:S(2)}, u32[]{:S(2)}) collective-permute-start(bf16[256,512]{1,0:T(8,128)(2,1)S(1)} %get-tuple-element.442.refs_0_), channel_id=1, source_target_pairs={{0,1},{1,0},{2,3},{3,2},{4,5},{5,4},{6,7},{7,6},{8,9},{9,8},{10,11... | collective-permute-start | bytes 786440 | tf_op jit(solution)/shard_map/ppermute | solution.py:572
  63.3 18.7 %collective-permute-start.35 = (bf16[256,512]{1,0:T(8,128)(2,1)S(1)}, bf16[256,512]{1,0:T(8,128)(2,1)S(1)}, u32[]{:S(2)}, u32[]{:S(2)}) collective-permute-start(bf16[256,512]{1,0:T(8,128)(2,1)S(1)} %collective-permute-done.34.refs_2_), channel_id=1, source_target_pairs={{0,1},{1,0},{2,3},{3,2},{4,5},{5,4},{6,7},{7,6},{8,9},{9,8},{10,11... | collective-permute-start | bytes 786440 | tf_op jit(solution)/shard_map/ppermute | solution.py:572
  67.3 30.8 %collective-permute-start.40 = (bf16[256,512]{1,0:T(8,128)(2,1)}, bf16[256,512]{1,0:T(8,128)(2,1)}, u32[]{:S(2)}, u32[]{:S(2)}) collective-permute-start(bf16[256,512]{1,0:T(8,128)(2,1)} %get-tuple-element.452.g_ref), channel_id=1, source_target_pairs={{0,2},{1,3},{2,0},{3,1},{4,6},{5,7},{6,4},{7,5},{8,10},{9,11},{10,... | collective-permute-start | bytes 786440 | tf_op jit(solution)/shard_map/ppermute | solution.py:572
  69.8 47.6 %collective-permute-start.39 = (bf16[256,512]{1,0:T(8,128)(2,1)}, bf16[256,512]{1,0:T(8,128)(2,1)S(1)}, u32[]{:S(2)}, u32[]{:S(2)}) collective-permute-start(bf16[256,512]{1,0:T(8,128)(2,1)} %get-tuple-element.452.g_ref), channel_id=1, source_target_pairs={{0,1},{1,0},{2,3},{3,2},{4,5},{5,4},{6,7},{7,6},{8,9},{9,8},{10,11... | collective-permute-start | bytes 786440 | tf_op jit(solution)/shard_map/ppermute | solution.py:572
  88.3 9.7 %collective-permute-start.20 = (bf16[64,2048]{1,0:T(8,128)(2,1)}, bf16[64,2048]{1,0:T(8,128)(2,1)}, u32[]{:S(2)}, u32[]{:S(2)}) collective-permute-start(bf16[64,2048]{1,0:T(8,128)(2,1)} %get-tuple-element.321), channel_id=1, source_target_pairs={{0,28},{4,24},{8,20},{12,16},{16,12},{20,8},{24,4},{28,0},{1,29},{... | collective-permute-start | bytes 786440 | tf_op jit(solution)/shard_map/cond/branch_6_fun/ppermute | solution.py:563
  98.1 19.2 %copy-start.2 = (bf16[2048,2048]{1,0:T(8,128)(2,1)S(1)}, bf16[2048,2048]{1,0:T(8,128)(2,1)}, u32[]{:S(2)}) copy-start(bf16[2048,2048]{1,0:T(8,128)(2,1)} %get-tuple-element.447.u_hbm) | copy-start | bytes 25165828
  98.1 19.2 %copy-start.3 = (bf16[2048,256]{1,0:T(8,128)(2,1)S(1)}, bf16[2048,256]{1,0:T(8,128)(2,1)}, u32[]{:S(2)}) copy-start(bf16[2048,256]{1,0:T(8,128)(2,1)} %get-tuple-element.451) | copy-start | bytes 3145732
  98.1 19.3 %copy-start.4 = (bf16[256,512]{1,0:T(8,128)(2,1)S(1)}, bf16[256,512]{1,0:T(8,128)(2,1)}, u32[]{:S(2)}) copy-start(bf16[256,512]{1,0:T(8,128)(2,1)} %get-tuple-element.452.g_ref) | copy-start | bytes 786436
  98.1 19.2 %collective-permute-start.41 = (bf16[256,512]{1,0:T(8,128)(2,1)}, bf16[256,512]{1,0:T(8,128)(2,1)S(1)}, u32[]{:S(2)}, u32[]{:S(2)}) collective-permute-start(bf16[256,512]{1,0:T(8,128)(2,1)} %collective-permute-done.40), channel_id=1, source_target_pairs={{0,1},{1,0},{2,3},{3,2},{4,5},{5,4},{6,7},{7,6},{8,9},{9,8},{10,11... | collective-permute-start | bytes 786440 | tf_op jit(solution)/shard_map/ppermute | solution.py:572
  98.2 11.5 %collective-permute-start.37 = (bf16[64,768]{1,0:T(8,128)(2,1)S(1)}, bf16[64,768]{1,0:T(8,128)(2,1)S(1)}, u32[]{:S(2)}, u32[]{:S(2)}) collective-permute-start(bf16[64,768]{1,0:T(8,128)(2,1)S(1)} %differ_later.1.refs_0_), channel_id=1, source_target_pairs={{0,1},{1,0},{2,3},{3,2},{4,5},{5,4},{6,7},{7,6},{8,9},{9,8},{10,11... | collective-permute-start | bytes 294920 | tf_op jit(solution)/shard_map/ppermute | solution.py:572
  100.2 10.6 %collective-permute-start.38 = (bf16[64,768]{1,0:T(8,128)(2,1)S(1)}, bf16[64,768]{1,0:T(8,128)(2,1)S(1)}, u32[]{:S(2)}, u32[]{:S(2)}) collective-permute-start(bf16[64,768]{1,0:T(8,128)(2,1)S(1)} %collective-permute-done.36.refs_2_), channel_id=1, source_target_pairs={{0,1},{1,0},{2,3},{3,2},{4,5},{5,4},{6,7},{7,6},{8,9},{9,8},{10,11... | collective-permute-start | bytes 294920 | tf_op jit(solution)/shard_map/ppermute | solution.py:572
  117.4 8.6 %collective-permute-start.24 = (bf16[64,2048]{1,0:T(8,128)(2,1)S(1)}, bf16[64,2048]{1,0:T(8,128)(2,1)}, u32[]{:S(2)}, u32[]{:S(2)}) collective-permute-start(bf16[64,2048]{1,0:T(8,128)(2,1)S(1)} %get-tuple-element.362), channel_id=1, source_target_pairs={{0,16},{4,20},{8,24},{12,28},{16,0},{20,4},{24,8},{28,12},{1,17},{... | collective-permute-start | bytes 786440 | tf_op jit(solution)/shard_map/cond/branch_3_fun/ppermute | solution.py:563
